TPU v7x, 32 devices: a whole 2x2x4 slice. The times are simulated.
32 devices in a mesh: tau: 2 (over y), aux: 16 (over z, x, core).
Axes of the slice: x: 2, y: 2, z: 4, core: 2. Of those that a mesh axis runs over, the one named last changes fastest.
Arguments:
- coefficients: bfloat16 [16384, 2048], P('aux'), may hold values from -0.125 to 0.125
- green_occ: bfloat16 [16, 2048, 2048], P('tau', 'aux'), may hold values from -6 to 6
- green_vir: bfloat16 [16, 2048, 2048], P('tau', 'aux'), may hold values from -6 to 6
- minimax: float32 [16, 16], replicated, may hold values from -1.5 to 1.5
- coulomb: float32 [512], replicated, may hold values from 0.006 to 0.04
Outputs:
- screened: float32 [16, 16384, 512], P('tau', 'aux')
All inputs are finite; a program needn't handle non-finite values.
Results may differ from a plain program's by a relative error of at most 0.0078.
Values may be sent and summed in bfloat16 or wider, within the bound.
No kernel may reach another device: no remote copies, remote signals or barrier semaphores. Data moves between devices by JAX's collectives and lax.ppermute only.
A program may use at most 128 MiB of HBM per device.

v0:
```python
import functools

import jax
import jax.numpy as jnp
from jax import lax
from jax.experimental import pallas as pl
from jax.experimental.pallas import tpu as pltpu
from jax.sharding import PartitionSpec as P

BF16 = jnp.bfloat16
F32 = jnp.float32
HBM = pl.BlockSpec(memory_space=pl.ANY)
VMEM = pl.BlockSpec(memory_space=pltpu.MemorySpace.VMEM)
NT = (((1,), (1,)), ((), ()))
MIB = 1 << 20


def room(mib):
    return pltpu.CompilerParams(vmem_limit_bytes=mib * MIB)

STRIP = 16


def dot(a, b):
    return jnp.dot(a, b, preferred_element_type=F32)


def ring_tables(size):
    chips = size // 2
    order = [2 * z for z in range(chips // 2)] + [2 * z + 1 for z in reversed(range(chips // 2))]
    ahead = [
        (2 * order[i] + core, 2 * order[(i + 1) % chips] + core)
        for i in range(chips)
        for core in range(2)
    ]
    behind = [(b, a) for a, b in ahead]
    cores = [(i, i ^ 1) for i in range(size)]
    return ahead, behind, cores


class Ring:
    def __init__(self, size, own, forward):
        self.chips = size // 2
        half = self.chips // 2
        self.far = half if forward else self.chips - 1 - half
        self.near = self.chips - 1 - self.far
        self.ahead, self.behind, self.cores = ring_tables(size)
        self.held, self.pairs = {0: own}, {}

    def swap(self, step):
        self.pairs[step] = lax.ppermute(self.held[step], "aux", self.cores)

    def go(self, step):
        way = self.ahead if step > 0 else self.behind
        before = step - 1 if step > 0 else step + 1
        self.held[step] = lax.ppermute(self.held[before], "aux", way)


def ring_steps(chips, forward):
    far = chips // 2 if forward else chips - 1 - chips // 2
    return [0] + list(range(1, far + 1)) + [-s for s in range(1, chips - far)]


def owners_of(chips, steps):
    me = lax.axis_index("aux")
    chip, core = me // 2, me % 2
    level, side = chip // 2, chip % 2
    place = jnp.where(side == 0, level, chips - 1 - level)
    source = (place - jnp.repeat(jnp.asarray(steps, jnp.int32), 2) + chips) % chips
    owner = jnp.where(source < chips // 2, 2 * source, 2 * (chips - 1 - source) + 1)
    return (2 * owner + (core + jnp.arange(2 * len(steps)) % 2) % 2).astype(jnp.int32)


def product_kernel(a, b, out):
    out[...] = (a[...].astype(F32) * b[...].astype(F32)).astype(BF16)


def pair_product(occ, vir, parts):
    times, rows, points = occ.shape
    each = times // parts
    occ, vir = (pltpu.with_memory_space_constraint(v, pltpu.HBM) for v in (occ, vir))
    outs = []
    for part in range(parts):
        spec = pl.BlockSpec((1, rows, points), lambda i, part=part: (part * each + i, 0, 0))
        outs.append(
            pl.pallas_call(
                product_kernel,
                out_shape=jax.ShapeDtypeStruct((each, rows, points), BF16),
                grid=(each,),
                in_specs=[spec, spec],
                out_specs=pl.BlockSpec((1, rows, points), lambda i: (i, 0, 0)),
                compiler_params=room(8),
                name="product",
            )(occ, vir)
        )
    return outs


def fold_kernel(halves, *refs):
    products, pieces, out = refs[:halves], refs[halves:-1], refs[-1]
    right = jnp.concatenate([p[...] for p in pieces], axis=0)
    done = 0
    for product in products:
        times, rows, points = product.shape
        left = product[...].reshape(times * rows, points)
        value = lax.dot_general(left, right, NT, preferred_element_type=F32)
        out[done : done + times] = value.astype(BF16).reshape(times, rows, right.shape[0])
        done += times


def fold(products, pieces):
    rows = products[0].shape[1]
    times = sum(p.shape[0] for p in products)
    width = sum(p.shape[0] for p in pieces)
    return pl.pallas_call(
        functools.partial(fold_kernel, len(products)),
        out_shape=jax.ShapeDtypeStruct((times, rows, width), BF16),
        in_specs=[VMEM] * (len(products) + len(pieces)),
        out_specs=VMEM,
        compiler_params=room(12),
        name="fold",
    )(*products, *pieces)


def panel_kernel(owners, row, *refs):
    pieces, panel, column = refs[:-2], refs[-2], refs[-1]
    depth = pieces[0].shape[0]
    for i, piece in enumerate(pieces):
        panel[pl.ds(pl.multiple_of(owners[i] * depth, depth), depth), :] = piece[...]
    size = row.shape[1]
    down = lax.broadcasted_iota(jnp.int32, (size, size), 0)
    across = lax.broadcasted_iota(jnp.int32, (size, size), 1)
    spread = jnp.where(down == across, jnp.broadcast_to(row[...], (size, size)), 0.0)
    column[...] = jnp.sum(spread, axis=1, keepdims=True)


def assemble(pieces, owners, coulomb):
    depth, points = pieces[0].shape
    size = depth * len(pieces)
    return pl.pallas_call(
        panel_kernel,
        out_shape=[
            jax.ShapeDtypeStruct((size, points), BF16),
            jax.ShapeDtypeStruct((size, 1), F32),
        ],
        in_specs=[pl.BlockSpec(memory_space=pltpu.SMEM)] + [VMEM] * (1 + len(pieces)),
        out_specs=[VMEM, VMEM],
        compiler_params=room(8),
        name="panel",
    )(owners, coulomb[None, :], *pieces)


def mix_weights(minimax, planes):
    place = lax.axis_index("tau")
    freqs, times = minimax.shape[0] // planes, minimax.shape[1] // planes
    tall, wide = freqs * STRIP, minimax.shape[1] * STRIP
    row, column = jnp.arange(tall), jnp.arange(wide)
    time = column // STRIP
    source = ((place + time // times) % planes) * times + time % times
    left = (row[:, None] // STRIP + place * freqs == jnp.arange(minimax.shape[0])).astype(F32)
    right = (source[None, :] == jnp.arange(minimax.shape[1])[:, None]).astype(F32)
    exact = lax.Precision.HIGHEST
    spread = jnp.dot(jnp.dot(left, minimax, precision=exact), right, precision=exact)
    spread = jnp.where(row[:, None] % STRIP == column[None, :] % STRIP, spread, 0.0)
    high = lax.reduce_precision(spread, 8, 7)
    rest = spread - high
    middle = lax.reduce_precision(rest, 8, 7)
    return jnp.concatenate([high, middle, rest - middle], axis=0).astype(BF16)


def mix_kernel(groups, parts, weights, order, *refs):
    folded, outs, total = refs[: groups * parts], refs[groups * parts : -1], refs[-1]
    times, rows, width = folded[0].shape
    tall = weights.shape[0] // 3
    freqs = tall // STRIP
    for strip in range(rows // STRIP):
        at = slice(strip * STRIP, (strip + 1) * STRIP)
        right = jnp.concatenate(
            [
                jnp.concatenate(
                    [
                        folded[g * parts + p][:, at, :].reshape(times * STRIP, width)
                        for p in range(parts)
                    ],
                    axis=1,
                )
                for g in range(groups)
            ],
            axis=0,
        )
        three = dot(weights[...], right)
        value = three[:tall] + (three[tall : 2 * tall] + three[2 * tall :])
        total[:, at, :] = value.astype(BF16).reshape(freqs, STRIP, width * parts)
    placed = dot(total[...].reshape(freqs * rows, width * parts), order[...])
    placed = placed.astype(BF16).reshape(freqs, rows, width * parts)
    first = 0
    for out in outs:
        out[...] = placed[first : first + out.shape[0]]
        first += out.shape[0]


def mix(folded, weights, order, sizes):
    times, rows, width = folded[0][0].shape
    parts = len(folded[0])
    panel = width * parts
    return pl.pallas_call(
        functools.partial(mix_kernel, len(folded), parts),
        out_shape=[jax.ShapeDtypeStruct((each, rows, panel), BF16) for each in sizes],
        in_specs=[VMEM] * (len(folded) * parts + 2),
        out_specs=[VMEM] * len(sizes),
        scratch_shapes=[pltpu.VMEM((sum(sizes), rows, panel), BF16)],
        compiler_params=room(16),
        name="mix",
    )(weights, order, *[f for g in folded for f in g])


GAIN = 2
TOKEN = jax.ShapeDtypeStruct((8, 128), F32)


def columns(ref, chip, wide):
    if len(ref.shape) == 3:
        return ref[chip]
    return ref[:, pl.ds(pl.multiple_of(chip * wide, wide), wide)]


def gain_kernel(places, fresh, owners, coef, panel, *refs):
    count = 2 * len(places)
    pieces, refs = refs[:count], refs[count:]
    before, (chi, step, slots) = refs[: len(refs) - 3], refs[len(refs) - 3 :]
    each, depth, size = pieces[0].shape
    wide = 2 * depth

    def one_frequency(w, carry):
        slot = slots.at[w]
        for j, place in enumerate(places):
            even = lax.rem(owners[2 * place], 2) == 0
            mine, theirs = pieces[2 * j][w], pieces[2 * j + 1][w]
            slot[j * wide : j * wide + depth, :] = jnp.where(even, mine, theirs)
            slot[j * wide + depth : (j + 1) * wide, :] = jnp.where(even, theirs, mine)
        for left, out, old in ((panel, step, 1), (coef, chi, 0)):
            total = None if fresh else before[old][w]
            for j, place in enumerate(places):
                chip = owners[2 * place] // 2
                term = dot(columns(left, chip, wide), slot[j * wide : (j + 1) * wide, :])
                total = term if total is None else total + term
            out[w] = total
        return carry

    lax.fori_loop(0, each, one_frequency, 0)


def gain(coef, panel, pieces, owners, places, before):
    each, depth, size = pieces[0].shape
    rows = coef.shape[-2]
    return pl.pallas_call(
        functools.partial(gain_kernel, places, not before),
        out_shape=[
            jax.ShapeDtypeStruct((each, rows, size), F32),
            jax.ShapeDtypeStruct((each, panel.shape[-2], size), F32),
        ],
        in_specs=[pl.BlockSpec(memory_space=pltpu.SMEM)] + [VMEM] * (2 + len(pieces) + len(before)),
        out_specs=[VMEM] * 2,
        scratch_shapes=[pltpu.VMEM((each, 2 * depth * len(places), size), BF16)],
        input_output_aliases={3 + len(pieces) + i: i for i in range(len(before))},
        compiler_params=room(20),
        name="gain",
    )(owners, coef, panel, *pieces, *before)


def close_kernel(first, aliased, column, chi, step, *refs):
    out, token, result, sems = refs[aliased:]
    token[...] = jnp.zeros_like(token)
    each, rows, size = chi.shape
    cuts = sems.shape[1]
    part = rows // cuts

    def write(w, i):
        cut = slice(i * part, (i + 1) * part)
        return pltpu.make_async_copy(result.at[w, cut], out.at[first + w, cut], sems.at[w, i])

    def one_frequency(w, carry):
        one = step[w] * column[...]
        low = one.astype(BF16)
        two = dot(low, low)
        pair = one + two
        series = (pair + dot(two.astype(BF16), pair.astype(BF16))).astype(BF16)
        for i in range(cuts):
            cut = slice(i * part, (i + 1) * part)
            value = chi[w, cut, :]
            result[w, cut, :] = value + dot(value.astype(BF16), series)
            write(w, i).start()
        return carry

    lax.fori_loop(0, each, one_frequency, 0)
    for w in range(each):
        for i in range(cuts):
            write(w, i).wait()


def close(column, chi, step, total, first, before, mark):
    each, rows, size = chi.shape
    extra = [] if before is None else [before, mark]
    cuts = 4
    return pl.pallas_call(
        functools.partial(close_kernel, first, len(extra)),
        out_shape=[jax.ShapeDtypeStruct((total, rows, size), F32), TOKEN],
        in_specs=[VMEM] * 3 + [HBM] * len(extra),
        out_specs=[HBM, VMEM],
        scratch_shapes=[
            pltpu.VMEM((each, rows, size), F32),
            pltpu.SemaphoreType.DMA((each, cuts)),
        ],
        input_output_aliases={} if before is None else {3: 0},
        compiler_params=room(24),
        name="close",
    )(column, chi, step, *extra)


def chunk_sizes(freqs):
    return SIZES[freqs] if freqs in SIZES else [1] * freqs


SIZES = {8: [4, 4]}
STREAMS = 1


def per_device(coefficients, green_occ, green_vir, minimax, coulomb):
    size, planes = lax.axis_size("aux"), lax.axis_size("tau")
    rows, points = coefficients.shape
    panel_size = coulomb.shape[0]
    depth = panel_size // size
    chips = size // 2
    freqs = minimax.shape[0] // planes
    sizes = chunk_sizes(freqs)
    shifts = [[((i + j) % planes, i) for i in range(planes)] for j in range(1, planes)]

    local = coefficients.reshape(depth, rows // depth, points)[:, 0, :]
    panel_ring = Ring(size, local, True)
    panel_ring.swap(0)
    product = pair_product(green_occ, green_vir, 2 if green_occ.shape[0] % 2 == 0 else 1)
    steps = [
        [r, -r] if r <= panel_ring.near else [r, 0] for r in range(1, panel_ring.far + 1)
    ]
    mine, theirs = [], []
    order = [s for group in steps for s in group]
    natural = jnp.repeat(owners_of(chips, order), depth) * depth + jnp.arange(panel_size) % depth
    early = {
        "weights": mix_weights(minimax, planes),
        "panel": owners_of(chips, order),
        "placing": (natural[:, None] == jnp.arange(panel_size)[None, :]).astype(BF16),
    }
    for way in (True, False):
        early[way] = owners_of(chips, ring_steps(chips, way))

    def fold_group(group):
        pieces = [p for s in group for p in (panel_ring.held[s], panel_ring.pairs[s])]
        if len(mine) > 1:
            together([(theirs[len(mine) - 2], k) for k in range(len(shifts))] + [(product, 0)])
        mine.append(fold(product, pieces))
        theirs.append([lax.ppermute(mine[-1], "tau", shift) for shift in shifts])

    for number in range(len(steps) + 1):
        group = steps[number] if number < len(steps) else []
        if number and group:
            sync = [(panel_ring.held, s) for s in steps[number - 1]]
            if number == 1:
                sync += [(early, key) for key in early] + [(product, 0)]
            if number == 2:
                sync += [(product, len(product) - 1)]
            if mine:
                sync += [(mine, len(mine) - 1)]
            together(sync)
        for step in group:
            if step:
                panel_ring.go(step)
        if number:
            for step in steps[number - 1]:
                if step:
                    panel_ring.swap(step)
            fold_group(steps[number - 1])
    groups = [[m] + t for m, t in zip(mine, theirs)]
    panel_pieces = [p for s in order for p in (panel_ring.held[s], panel_ring.pairs[s])]
    panel = list(assemble(panel_pieces, early["panel"], coulomb))
    chunks = mix([list(g) for g in zip(*groups)], early["weights"], early["placing"], sizes)

    rings, outs, marks = [], [None], []
    lanes = min(STREAMS, len(chunks))
    ups, downs = [[] for _ in range(lanes)], [[] for _ in range(lanes)]
    ways = {}
    for i, chunk in enumerate(chunks):
        lane = i % lanes
        ways[i] = (i // lanes + lane) % 2 == 0
        ring = Ring(size, chunk, ways[i])
        rings.append(ring)
        ups[lane] += [(i, s) for s in range(1, ring.far + 1)]
        downs[lane] += [(i, -s) for s in range(1, ring.near + 1)]
    plan = []
    for n in range(max(len(m) for m in ups + downs)):
        for lane in range(lanes):
            moves = [m[lane][n] for m in (ups, downs) if n < len(m[lane])]
            plan.append(moves)
    count = len(plan)
    points_of_chip = points // chips
    left = coefficients
    if points_of_chip % 128:
        left = jnp.swapaxes(left.reshape(rows, chips, points_of_chip), 0, 1)
        panel[0] = jnp.swapaxes(panel[0].reshape(panel_size, chips, points_of_chip), 0, 1)
    sums, summed = {}, {c: 0 for c in range(len(rings))}

    def add(c, steps):
        listed = ring_steps(chips, ways[c])
        pieces = [p for s in steps for p in (rings[c].held[s], rings[c].pairs[s])]
        places = tuple(listed.index(s) for s in steps)
        chi, step = gain(
            left, panel[0], pieces, early[ways[c]], places, sums.get(c, [])
        )
        sums[c] = [chi, step]
        summed[c] += len(steps)
        if summed[c] == chips:
            outs[0], mark = close(
                panel[1], chi, step, freqs, sum(sizes[:c]), outs[0], marks[-1] if marks else None
            )
            marks.append(mark)

    waiting, swapped = {c: [] for c in range(len(rings))}, []

    def add_waiting():
        for c in range(len(rings)):
            last = summed[c] + len(waiting[c]) == chips
            while len(waiting[c]) >= GAIN or (last and waiting[c]):
                add(c, waiting[c][:GAIN])
                del waiting[c][:GAIN]

    for number in range(count + 1):
        moves = plan[number] if number < count else []
        landed = plan[number - 1] if number else []
        sources = [(i, s - 1 if s > 0 else s + 1) for i, s in moves]
        started = [(i, s) for i, s in dict.fromkeys(sources) if s == 0 and not rings[i].pairs]
        sync = [(rings[i].held, s) for i, s in dict.fromkeys(sources + landed)]
        sync += [(rings[i].pairs, s) for i, s in swapped]
        if number == 1:
            sync += [(panel, 0), (panel, 1)]
        sync += [(sums[c], k) for c in sums for k in range(2) if summed[c] < chips]
        if marks and summed[len(rings) - 1] < chips:
            sync += [(marks, len(marks) - 1)]
        if number < count:
            together(sync)
        for i, s in moves:
            rings[i].go(s)
        before = dict(summed)
        add_waiting()
        now = list(dict.fromkeys(started + landed))
        grown = [c for c in sums if before[c] < summed[c] < chips]
        if grown and moves:
            together([(rings[i].held, s) for i, s in now] + [(sums[c], k) for c in grown for k in range(2)])
        for i, s in now:
            rings[i].swap(s)
            waiting[i].append(s)
        swapped = now
        if number >= count - 1:
            swapped = []
            add_waiting()
    return outs[0]


def together(sync):
    values = lax.optimization_barrier(tuple(box[key] for box, key in sync))
    for (box, key), value in zip(sync, values):
        box[key] = value


def solution(mesh):
    placed = (P("aux", None), P("tau", "aux", None), P("tau", "aux", None), P(), P())
    return jax.shard_map(
        per_device, mesh=mesh, in_specs=placed, out_specs=P("tau", "aux", None), check_vma=False
    )
```

profile of v0, /device:TPU:0, one launch (start us, length us, event | category | flops | bytes accessed | tf_op | source)
XLA Modules:
  0.0 172.9 jit_solution(434873451209650925)
XLA Ops:
  1.5 3.0 %collective-permute-start.1 = (bf16[32,2048]{1,0:T(8,128)(2,1)S(1)}, bf16[32,2048]{1,0:T(8,128)(2,1)S(1)}, u32[]{:S(2)}, u32[]{:S(2)}) collective-permute-start(bf16[32,2048]{1,0:T(8,128)(2,1)S(1)} %bitcast.8), channel_id=1, source_target_pairs={{4,0},{5,1},{8,4},{9,5},{12,8},{13,9},{14,12},{15,13},{10,14},{11,... | collective-permute-start | bytes 393224 | tf_op jit(solution)/shard_map/ppermute | solution.py:56
  8.0 3.2 %product.2.refs_0_ = bf16[4,128,2048]{2,1,0:T(8,128)(2,1)S(1)} custom-call(bf16[8,128,2048]{2,1,0:T(8,128)(2,1)} %a.3, bf16[8,128,2048]{2,1,0:T(8,128)(2,1)} %b.3), custom_call_target="tpu_custom_call" | custom-call | tf_op jit(solution)/shard_map/product/pallas_call | solution.py:86
  11.8 2.0 %collective-permute-start.2 = (bf16[32,2048]{1,0:T(8,128)(2,1)S(1)}, bf16[32,2048]{1,0:T(8,128)(2,1)S(1)}, u32[]{:S(2)}, u32[]{:S(2)}) collective-permute-start(bf16[32,2048]{1,0:T(8,128)(2,1)S(1)} %collective-permute-done.refs_2_.refs_0_), channel_id=1, source_target_pairs={{0,4},{1,5},{4,8},{5,9},{8,12},{9,13},{12,14},{13,15},{14,10},{15,... | collective-permute-start | bytes 393224 | tf_op jit(solution)/shard_map/ppermute | solution.py:56
  13.8 3.1 %product.3.refs_1_ = bf16[4,128,2048]{2,1,0:T(8,128)(2,1)S(1)} custom-call(bf16[8,128,2048]{2,1,0:T(8,128)(2,1)} %a.3, bf16[8,128,2048]{2,1,0:T(8,128)(2,1)} %b.3), custom_call_target="tpu_custom_call" | custom-call | tf_op jit(solution)/shard_map/product/pallas_call | solution.py:86
  28.3 2.9 %collective-permute-done.14.refs_2_.refs_12_ = bf16[32,2048]{1,0:T(8,128)(2,1)S(1)} collective-permute-done((bf16[32,2048]{1,0:T(8,128)(2,1)S(1)}, bf16[32,2048]{1,0:T(8,128)(2,1)S(1)}, u32[]{:S(2)}, u32[]{:S(2)}) %collective-permute-start.14) | collective-permute-done | bytes 131104 | tf_op jit(solution)/shard_map/ppermute | solution.py:56
  37.6 4.6 %collective-permute-done.17.refs_6_ = bf16[8,128,128]{2,1,0:T(8,128)(2,1)S(1)} collective-permute-done((bf16[8,128,128]{2,1,0:T(8,128)(2,1)S(1)}, bf16[8,128,128]{2,1,0:T(8,128)(2,1)S(1)}, u32[]{:S(2)}, u32[]{:S(2)}) %collective-permute-start.17) | collective-permute-done | bytes 262176 | tf_op jit(solution)/shard_map/ppermute | solution.py:361
  42.2 4.7 %collective-permute-done.18.refs_7_ = bf16[8,128,128]{2,1,0:T(8,128)(2,1)S(1)} collective-permute-done((bf16[8,128,128]{2,1,0:T(8,128)(2,1)S(1)}, bf16[8,128,128]{2,1,0:T(8,128)(2,1)S(1)}, u32[]{:S(2)}, u32[]{:S(2)}) %collective-permute-start.18) | collective-permute-done | bytes 262176 | tf_op jit(solution)/shard_map/ppermute | solution.py:361
  46.9 1.6 mix.1
  51.4 11.5 %collective-permute-done.20.refs_0_ = bf16[4,128,512]{2,1,0:T(8,128)(2,1)S(1)} collective-permute-done((bf16[4,128,512]{2,1,0:T(8,128)(2,1)S(1)}, bf16[4,128,512]{2,1,0:T(8,128)(2,1)S(1)}, u32[]{:S(2)}, u32[]{:S(2)}) %collective-permute-start.20) | collective-permute-done | bytes 524320 | tf_op jit(solution)/shard_map/ppermute | solution.py:56
  65.6 12.1 %collective-permute-done.22.refs_2_ = bf16[4,128,512]{2,1,0:T(8,128)(2,1)S(1)} collective-permute-done((bf16[4,128,512]{2,1,0:T(8,128)(2,1)S(1)}, bf16[4,128,512]{2,1,0:T(8,128)(2,1)S(1)}, u32[]{:S(2)}, u32[]{:S(2)}) %collective-permute-start.22) | collective-permute-done | bytes 524320 | tf_op jit(solution)/shard_map/ppermute | solution.py:56
  81.0 4.5 %gain.8 = (f32[4,1024,512]{2,1,0:T(8,128)S(1)}, f32[4,512,512]{2,1,0:T(8,128)S(1)}) custom-call(s32[16]{0:T(128)S(1)} %get-tuple-element.133.owners, bf16[1024,2048]{1,0:T(8,128)(2,1)S(1)} %copy-done.2, bf16[512,2048]{1,0:T(8,128)(2,1)S(1)} %get-tuple-element.127.panel, bf16[4,128,512]{2,1,0:T(8,128)(2,1)S(1)} %get-tuple-element.121.refs_0_, ...), custom_call_target="tpu_custom_call" | custom-call | tf_op jit(solution)/shard_map/gain/pallas_call | solution.py:256
  86.1 6.1 %collective-permute-done.26.refs_2_ = bf16[4,128,512]{2,1,0:T(8,128)(2,1)S(1)} collective-permute-done((bf16[4,128,512]{2,1,0:T(8,128)(2,1)S(1)}, bf16[4,128,512]{2,1,0:T(8,128)(2,1)S(1)}, u32[]{:S(2)}, u32[]{:S(2)}) %collective-permute-start.26) | collective-permute-done | bytes 524320 | tf_op jit(solution)/shard_map/ppermute | solution.py:56
  95.6 5.4 %gain.9 = (f32[4,1024,512]{2,1,0:T(8,128)S(1)}, f32[4,512,512]{2,1,0:T(8,128)S(1)}) custom-call(s32[16]{0:T(128)S(1)} %get-tuple-element.133.owners, bf16[1024,2048]{1,0:T(8,128)(2,1)S(1)} %copy-done.2, bf16[512,2048]{1,0:T(8,128)(2,1)S(1)} %get-tuple-element.127.panel, ...), custom_call_target="tpu_custom_call", output_to_operand_aliasing={{0}: (7, {}), {1}: (8, {})} | custom-call | tf_op jit(solution)/shard_map/gain/pallas_call | solution.py:256
  101.6 4.0 %collective-permute-done.30.refs_2_ = bf16[4,128,512]{2,1,0:T(8,128)(2,1)S(1)} collective-permute-done((bf16[4,128,512]{2,1,0:T(8,128)(2,1)S(1)}, bf16[4,128,512]{2,1,0:T(8,128)(2,1)S(1)}, u32[]{:S(2)}, u32[]{:S(2)}) %collective-permute-start.30) | collective-permute-done | bytes 524320 | tf_op jit(solution)/shard_map/ppermute | solution.py:56
  107.9 5.4 %gain.10 = (f32[4,1024,512]{2,1,0:T(8,128)S(1)}, f32[4,512,512]{2,1,0:T(8,128)S(1)}) custom-call(s32[16]{0:T(128)S(1)} %get-tuple-element.133.owners, bf16[1024,2048]{1,0:T(8,128)(2,1)S(1)} %copy-done.2, bf16[512,2048]{1,0:T(8,128)(2,1)S(1)} %get-tuple-element.127.panel, ...), custom_call_target="tpu_custom_call", output_to_operand_aliasing={{0}: (7, {}), {1}: (8, {})} | custom-call | tf_op jit(solution)/shard_map/gain/pallas_call | solution.py:256
  113.9 4.5 %collective-permute-done.35.refs_0_ = bf16[4,128,512]{2,1,0:T(8,128)(2,1)S(1)} collective-permute-done((bf16[4,128,512]{2,1,0:T(8,128)(2,1)S(1)}, bf16[4,128,512]{2,1,0:T(8,128)(2,1)S(1)}, u32[]{:S(2)}, u32[]{:S(2)}) %collective-permute-start.35) | collective-permute-done | bytes 524320 | tf_op jit(solution)/shard_map/ppermute | solution.py:56
  121.7 4.6 %gain.11 = (f32[4,1024,512]{2,1,0:T(8,128)S(1)}, f32[4,512,512]{2,1,0:T(8,128)S(1)}) custom-call(s32[16]{0:T(128)S(1)} %get-tuple-element.126.owners, bf16[1024,2048]{1,0:T(8,128)(2,1)S(1)} %copy-done.2, bf16[512,2048]{1,0:T(8,128)(2,1)S(1)} %get-tuple-element.127.panel, bf16[4,128,512]{2,1,0:T(8,128)(2,1)S(1)} %get-tuple-element.156.refs_0_, ...), custom_call_target="tpu_custom_call" | custom-call | tf_op jit(solution)/shard_map/gain/pallas_call | solution.py:256
  126.8 5.4 %gain.12 = (f32[4,1024,512]{2,1,0:T(8,128)S(1)}, f32[4,512,512]{2,1,0:T(8,128)S(1)}) custom-call(s32[16]{0:T(128)S(1)} %get-tuple-element.133.owners, bf16[1024,2048]{1,0:T(8,128)(2,1)S(1)} %copy-done.2, bf16[512,2048]{1,0:T(8,128)(2,1)S(1)} %get-tuple-element.127.panel, ...), custom_call_target="tpu_custom_call", output_to_operand_aliasing={{0}: (7, {}), {1}: (8, {})} | custom-call | tf_op jit(solution)/shard_map/gain/pallas_call | solution.py:256
  132.2 7.1 %close.2 = (f32[8,1024,512]{2,1,0:T(8,128)}, f32[8,128]{1,0:T(8,128)S(1)}) custom-call(f32[512,1]{1,0:T(8,128)S(1)} %get-tuple-element.125.column, f32[4,1024,512]{2,1,0:T(8,128)S(1)} %get-tuple-element.183.chi, f32[4,512,512]{2,1,0:T(8,128)S(1)} %get-tuple-element.184.step), custom_call_target="tpu_custom_call" | custom-call | tf_op jit(solution)/shard_map/close/pallas_call | solution.py:305
  141.4 5.3 %gain.13 = (f32[4,1024,512]{2,1,0:T(8,128)S(1)}, f32[4,512,512]{2,1,0:T(8,128)S(1)}) custom-call(s32[16]{0:T(128)S(1)} %get-tuple-element.126.owners, bf16[1024,2048]{1,0:T(8,128)(2,1)S(1)} %copy-done.2, bf16[512,2048]{1,0:T(8,128)(2,1)S(1)} %get-tuple-element.127.panel, ...), custom_call_target="tpu_custom_call", output_to_operand_aliasing={{0}: (7, {}), {1}: (8, {})} | custom-call | tf_op jit(solution)/shard_map/gain/pallas_call | solution.py:256
  147.3 6.0 %collective-permute-done.43.refs_0_ = bf16[4,128,512]{2,1,0:T(8,128)(2,1)S(1)} collective-permute-done((bf16[4,128,512]{2,1,0:T(8,128)(2,1)S(1)}, bf16[4,128,512]{2,1,0:T(8,128)(2,1)S(1)}, u32[]{:S(2)}, u32[]{:S(2)}) %collective-permute-start.43) | collective-permute-done | bytes 524320 | tf_op jit(solution)/shard_map/ppermute | solution.py:56
  154.3 5.3 %gain.14 = (f32[4,1024,512]{2,1,0:T(8,128)S(1)}, f32[4,512,512]{2,1,0:T(8,128)S(1)}) custom-call(s32[16]{0:T(128)S(1)} %get-tuple-element.126.owners, bf16[1024,2048]{1,0:T(8,128)(2,1)S(1)} %copy-done.2, bf16[512,2048]{1,0:T(8,128)(2,1)S(1)} %get-tuple-element.127.panel, ...), custom_call_target="tpu_custom_call", output_to_operand_aliasing={{0}: (7, {}), {1}: (8, {})} | custom-call | tf_op jit(solution)/shard_map/gain/pallas_call | solution.py:256
  159.7 5.4 %gain.15 = (f32[4,1024,512]{2,1,0:T(8,128)S(1)}, f32[4,512,512]{2,1,0:T(8,128)S(1)}) custom-call(s32[16]{0:T(128)S(1)} %get-tuple-element.126.owners, bf16[1024,2048]{1,0:T(8,128)(2,1)S(1)} %copy-done.2, bf16[512,2048]{1,0:T(8,128)(2,1)S(1)} %get-tuple-element.127.panel, ...), custom_call_target="tpu_custom_call", output_to_operand_aliasing={{0}: (7, {}), {1}: (8, {})} | custom-call | tf_op jit(solution)/shard_map/gain/pallas_call | solution.py:256
  165.0 7.7 %close.3 = (f32[8,1024,512]{2,1,0:T(8,128)}, f32[8,128]{1,0:T(8,128)}) custom-call(f32[512,1]{1,0:T(8,128)S(1)} %get-tuple-element.125.column, f32[4,1024,512]{2,1,0:T(8,128)S(1)} %get-tuple-element.200.chi, f32[4,512,512]{2,1,0:T(8,128)S(1)} %get-tuple-element.201.step, ...), custom_call_target="tpu_custom_call", output_to_operand_aliasing={{0}: (3, {})} | custom-call | tf_op jit(solution)/shard_map/close/pallas_call | solution.py:305
  (123 shorter events, 47.1 us)
Async XLA Ops:
  1.5 9.7 %collective-permute-start.1 = (bf16[32,2048]{1,0:T(8,128)(2,1)S(1)}, bf16[32,2048]{1,0:T(8,128)(2,1)S(1)}, u32[]{:S(2)}, u32[]{:S(2)}) collective-permute-start(bf16[32,2048]{1,0:T(8,128)(2,1)S(1)} %bitcast.8), channel_id=1, source_target_pairs={{4,0},{5,1},{8,4},{9,5},{12,8},{13,9},{14,12},{15,13},{10,14},{11,... | collective-permute-start | bytes 393224 | tf_op jit(solution)/shard_map/ppermute | solution.py:56
  21.5 9.7 %collective-permute-start.10 = (bf16[8,128,128]{2,1,0:T(8,128)(2,1)S(1)}, bf16[8,128,128]{2,1,0:T(8,128)(2,1)S(1)}, u32[]{:S(2)}, u32[]{:S(2)}) collective-permute-start(bf16[8,128,128]{2,1,0:T(8,128)(2,1)S(1)} %fold.4.refs_0_), channel_id=1, source_target_pairs={{16,0},{0,16},{17,1},{1,17},{18,2},{2,18},{19,3},{3,19},{20,4},{4,... | collective-permute-start | bytes 786440 | tf_op jit(solution)/shard_map/ppermute | solution.py:361
  24.3 10.5 %collective-permute-start.13 = (bf16[8,128,128]{2,1,0:T(8,128)(2,1)S(1)}, bf16[8,128,128]{2,1,0:T(8,128)(2,1)S(1)}, u32[]{:S(2)}, u32[]{:S(2)}) collective-permute-start(bf16[8,128,128]{2,1,0:T(8,128)(2,1)S(1)} %fold.5.refs_1_), channel_id=1, source_target_pairs={{16,0},{0,16},{17,1},{1,17},{18,2},{2,18},{19,3},{3,19},{20,4},{4,... | collective-permute-start | bytes 786440 | tf_op jit(solution)/shard_map/ppermute | solution.py:361
  33.0 9.2 %collective-permute-start.17 = (bf16[8,128,128]{2,1,0:T(8,128)(2,1)S(1)}, bf16[8,128,128]{2,1,0:T(8,128)(2,1)S(1)}, u32[]{:S(2)}, u32[]{:S(2)}) collective-permute-start(bf16[8,128,128]{2,1,0:T(8,128)(2,1)S(1)} %fold.6.refs_2_), channel_id=1, source_target_pairs={{16,0},{0,16},{17,1},{1,17},{18,2},{2,18},{19,3},{3,19},{20,4},{4,... | collective-permute-start | bytes 786440 | tf_op jit(solution)/shard_map/ppermute | solution.py:361
  36.0 10.8 %collective-permute-start.18 = (bf16[8,128,128]{2,1,0:T(8,128)(2,1)S(1)}, bf16[8,128,128]{2,1,0:T(8,128)(2,1)S(1)}, u32[]{:S(2)}, u32[]{:S(2)}) collective-permute-start(bf16[8,128,128]{2,1,0:T(8,128)(2,1)S(1)} %fold.7.refs_3_), channel_id=1, source_target_pairs={{16,0},{0,16},{17,1},{1,17},{18,2},{2,18},{19,3},{3,19},{20,4},{4,... | collective-permute-start | bytes 786440 | tf_op jit(solution)/shard_map/ppermute | solution.py:361
  48.6 14.3 %collective-permute-start.20 = (bf16[4,128,512]{2,1,0:T(8,128)(2,1)S(1)}, bf16[4,128,512]{2,1,0:T(8,128)(2,1)S(1)}, u32[]{:S(2)}, u32[]{:S(2)}) collective-permute-start(bf16[4,128,512]{2,1,0:T(8,128)(2,1)S(1)} %get-tuple-element.121.refs_0_), channel_id=1, source_target_pairs={{4,0},{5,1},{8,4},{9,5},{12,8},{13,9},{14,12},{15,13},{10,14},{11,... | collective-permute-start | bytes 1572872 | tf_op jit(solution)/shard_map/ppermute | solution.py:56
  49.3 14.0 %collective-permute-start.19 = (bf16[4,128,512]{2,1,0:T(8,128)(2,1)S(1)}, bf16[4,128,512]{2,1,0:T(8,128)(2,1)S(1)}, u32[]{:S(2)}, u32[]{:S(2)}) collective-permute-start(bf16[4,128,512]{2,1,0:T(8,128)(2,1)S(1)} %get-tuple-element.121.refs_0_), channel_id=1, source_target_pairs={{0,4},{1,5},{4,8},{5,9},{8,12},{9,13},{12,14},{13,15},{14,10},{15,... | collective-permute-start | bytes 1572872 | tf_op jit(solution)/shard_map/ppermute | solution.py:56
  63.3 14.3 %collective-permute-start.22 = (bf16[4,128,512]{2,1,0:T(8,128)(2,1)S(1)}, bf16[4,128,512]{2,1,0:T(8,128)(2,1)S(1)}, u32[]{:S(2)}, u32[]{:S(2)}) collective-permute-start(bf16[4,128,512]{2,1,0:T(8,128)(2,1)S(1)} %collective-permute-done.19.refs_2_), channel_id=1, source_target_pairs={{0,4},{1,5},{4,8},{5,9},{8,12},{9,13},{12,14},{13,15},{14,10},{15,... | collective-permute-start | bytes 1572872 | tf_op jit(solution)/shard_map/ppermute | solution.py:56
  64.6 13.0 %collective-permute-start.25 = (bf16[4,128,512]{2,1,0:T(8,128)(2,1)S(1)}, bf16[4,128,512]{2,1,0:T(8,128)(2,1)S(1)}, u32[]{:S(2)}, u32[]{:S(2)}) collective-permute-start(bf16[4,128,512]{2,1,0:T(8,128)(2,1)S(1)} %collective-permute-done.20.refs_0_), channel_id=1, source_target_pairs={{0,1},{1,0},{2,3},{3,2},{4,5},{5,4},{6,7},{7,6},{8,9},{9,8},{10,11... | collective-permute-start | bytes 1572872 | tf_op jit(solution)/shard_map/ppermute | solution.py:51
  64.9 14.1 %collective-permute-start.23 = (bf16[4,128,512]{2,1,0:T(8,128)(2,1)S(1)}, bf16[4,128,512]{2,1,0:T(8,128)(2,1)S(1)}, u32[]{:S(2)}, u32[]{:S(2)}) collective-permute-start(bf16[4,128,512]{2,1,0:T(8,128)(2,1)S(1)} %collective-permute-done.20.refs_0_), channel_id=1, source_target_pairs={{4,0},{5,1},{8,4},{9,5},{12,8},{13,9},{14,12},{15,13},{10,14},{11,... | collective-permute-start | bytes 1572872 | tf_op jit(solution)/shard_map/ppermute | solution.py:56
  79.0 13.3 %collective-permute-start.26 = (bf16[4,128,512]{2,1,0:T(8,128)(2,1)S(1)}, bf16[4,128,512]{2,1,0:T(8,128)(2,1)S(1)}, u32[]{:S(2)}, u32[]{:S(2)}) collective-permute-start(bf16[4,128,512]{2,1,0:T(8,128)(2,1)S(1)} %collective-permute-done.22.refs_2_), channel_id=1, source_target_pairs={{0,4},{1,5},{4,8},{5,9},{8,12},{9,13},{12,14},{13,15},{14,10},{15,... | collective-permute-start | bytes 1572872 | tf_op jit(solution)/shard_map/ppermute | solution.py:56
  80.5 13.0 %collective-permute-start.27 = (bf16[4,128,512]{2,1,0:T(8,128)(2,1)S(1)}, bf16[4,128,512]{2,1,0:T(8,128)(2,1)S(1)}, u32[]{:S(2)}, u32[]{:S(2)}) collective-permute-start(bf16[4,128,512]{2,1,0:T(8,128)(2,1)S(1)} %collective-permute-done.23.refs_0_), channel_id=1, source_target_pairs={{4,0},{5,1},{8,4},{9,5},{12,8},{13,9},{14,12},{15,13},{10,14},{11,... | collective-permute-start | bytes 1572872 | tf_op jit(solution)/shard_map/ppermute | solution.py:56
  85.6 8.0 %collective-permute-start.28 = (bf16[4,128,512]{2,1,0:T(8,128)(2,1)S(1)}, bf16[4,128,512]{2,1,0:T(8,128)(2,1)S(1)}, u32[]{:S(2)}, u32[]{:S(2)}) collective-permute-start(bf16[4,128,512]{2,1,0:T(8,128)(2,1)S(1)} %collective-permute-done.22.refs_2_), channel_id=1, source_target_pairs={{0,1},{1,0},{2,3},{3,2},{4,5},{5,4},{6,7},{7,6},{8,9},{9,8},{10,11... | collective-permute-start | bytes 1572872 | tf_op jit(solution)/shard_map/ppermute | solution.py:51
  85.6 7.9 %collective-permute-start.29 = (bf16[4,128,512]{2,1,0:T(8,128)(2,1)S(1)}, bf16[4,128,512]{2,1,0:T(8,128)(2,1)S(1)}, u32[]{:S(2)}, u32[]{:S(2)}) collective-permute-start(bf16[4,128,512]{2,1,0:T(8,128)(2,1)S(1)} %collective-permute-done.23.refs_0_), channel_id=1, source_target_pairs={{0,1},{1,0},{2,3},{3,2},{4,5},{5,4},{6,7},{7,6},{8,9},{9,8},{10,11... | collective-permute-start | bytes 1572872 | tf_op jit(solution)/shard_map/ppermute | solution.py:51
  93.5 12.1 %collective-permute-start.30 = (bf16[4,128,512]{2,1,0:T(8,128)(2,1)S(1)}, bf16[4,128,512]{2,1,0:T(8,128)(2,1)S(1)}, u32[]{:S(2)}, u32[]{:S(2)}) collective-permute-start(bf16[4,128,512]{2,1,0:T(8,128)(2,1)S(1)} %get-tuple-element.156.refs_0_), channel_id=1, source_target_pairs={{4,0},{5,1},{8,4},{9,5},{12,8},{13,9},{14,12},{15,13},{10,14},{11,... | collective-permute-start | bytes 1572872 | tf_op jit(solution)/shard_map/ppermute | solution.py:56
  94.0 11.8 %collective-permute-start.31 = (bf16[4,128,512]{2,1,0:T(8,128)(2,1)S(1)}, bf16[4,128,512]{2,1,0:T(8,128)(2,1)S(1)}, u32[]{:S(2)}, u32[]{:S(2)}) collective-permute-start(bf16[4,128,512]{2,1,0:T(8,128)(2,1)S(1)} %collective-permute-done.26.refs_2_), channel_id=1, source_target_pairs={{0,4},{1,5},{4,8},{5,9},{8,12},{9,13},{12,14},{13,15},{14,10},{15,... | collective-permute-start | bytes 1572872 | tf_op jit(solution)/shard_map/ppermute | solution.py:56
  105.8 12.6 %collective-permute-start.35 = (bf16[4,128,512]{2,1,0:T(8,128)(2,1)S(1)}, bf16[4,128,512]{2,1,0:T(8,128)(2,1)S(1)}, u32[]{:S(2)}, u32[]{:S(2)}) collective-permute-start(bf16[4,128,512]{2,1,0:T(8,128)(2,1)S(1)} %get-tuple-element.156.refs_0_), channel_id=1, source_target_pairs={{0,4},{1,5},{4,8},{5,9},{8,12},{9,13},{12,14},{13,15},{14,10},{15,... | collective-permute-start | bytes 1572872 | tf_op jit(solution)/shard_map/ppermute | solution.py:56
  107.5 12.2 %collective-permute-start.36 = (bf16[4,128,512]{2,1,0:T(8,128)(2,1)S(1)}, bf16[4,128,512]{2,1,0:T(8,128)(2,1)S(1)}, u32[]{:S(2)}, u32[]{:S(2)}) collective-permute-start(bf16[4,128,512]{2,1,0:T(8,128)(2,1)S(1)} %collective-permute-done.30.refs_2_), channel_id=1, source_target_pairs={{4,0},{5,1},{8,4},{9,5},{12,8},{13,9},{14,12},{15,13},{10,14},{11,... | collective-permute-start | bytes 1572872 | tf_op jit(solution)/shard_map/ppermute | solution.py:56
  119.7 19.7 %collective-permute-start.39 = (bf16[4,128,512]{2,1,0:T(8,128)(2,1)S(1)}, bf16[4,128,512]{2,1,0:T(8,128)(2,1)S(1)}, u32[]{:S(2)}, u32[]{:S(2)}) collective-permute-start(bf16[4,128,512]{2,1,0:T(8,128)(2,1)S(1)} %collective-permute-done.35.refs_0_), channel_id=1, source_target_pairs={{0,4},{1,5},{4,8},{5,9},{8,12},{9,13},{12,14},{13,15},{14,10},{15,... | collective-permute-start | bytes 1572872 | tf_op jit(solution)/shard_map/ppermute | solution.py:56
  121.0 18.3 %collective-permute-start.40 = (bf16[4,128,512]{2,1,0:T(8,128)(2,1)S(1)}, bf16[4,128,512]{2,1,0:T(8,128)(2,1)S(1)}, u32[]{:S(2)}, u32[]{:S(2)}) collective-permute-start(bf16[4,128,512]{2,1,0:T(8,128)(2,1)S(1)} %collective-permute-done.36.refs_2_), channel_id=1, source_target_pairs={{4,0},{5,1},{8,4},{9,5},{12,8},{13,9},{14,12},{15,13},{10,14},{11,... | collective-permute-start | bytes 1572872 | tf_op jit(solution)/shard_map/ppermute | solution.py:56
  126.3 13.1 %collective-permute-start.41 = (bf16[4,128,512]{2,1,0:T(8,128)(2,1)S(1)}, bf16[4,128,512]{2,1,0:T(8,128)(2,1)S(1)}, u32[]{:S(2)}, u32[]{:S(2)}) collective-permute-start(bf16[4,128,512]{2,1,0:T(8,128)(2,1)S(1)} %collective-permute-done.35.refs_0_), channel_id=1, source_target_pairs={{0,1},{1,0},{2,3},{3,2},{4,5},{5,4},{6,7},{7,6},{8,9},{9,8},{10,11... | collective-permute-start | bytes 1572872 | tf_op jit(solution)/shard_map/ppermute | solution.py:51
  126.3 13.0 %collective-permute-start.42 = (bf16[4,128,512]{2,1,0:T(8,128)(2,1)S(1)}, bf16[4,128,512]{2,1,0:T(8,128)(2,1)S(1)}, u32[]{:S(2)}, u32[]{:S(2)}) collective-permute-start(bf16[4,128,512]{2,1,0:T(8,128)(2,1)S(1)} %collective-permute-done.36.refs_2_), channel_id=1, source_target_pairs={{0,1},{1,0},{2,3},{3,2},{4,5},{5,4},{6,7},{7,6},{8,9},{9,8},{10,11... | collective-permute-start | bytes 1572872 | tf_op jit(solution)/shard_map/ppermute | solution.py:51
  139.3 14.0 %collective-permute-start.43 = (bf16[4,128,512]{2,1,0:T(8,128)(2,1)S(1)}, bf16[4,128,512]{2,1,0:T(8,128)(2,1)S(1)}, u32[]{:S(2)}, u32[]{:S(2)}) collective-permute-start(bf16[4,128,512]{2,1,0:T(8,128)(2,1)S(1)} %collective-permute-done.39.refs_0_), channel_id=1, source_target_pairs={{0,4},{1,5},{4,8},{5,9},{8,12},{9,13},{12,14},{13,15},{14,10},{15,... | collective-permute-start | bytes 1572872 | tf_op jit(solution)/shard_map/ppermute | solution.py:56
  140.7 13.6 %collective-permute-start.45 = (bf16[4,128,512]{2,1,0:T(8,128)(2,1)S(1)}, bf16[4,128,512]{2,1,0:T(8,128)(2,1)S(1)}, u32[]{:S(2)}, u32[]{:S(2)}) collective-permute-start(bf16[4,128,512]{2,1,0:T(8,128)(2,1)S(1)} %collective-permute-done.40.refs_2_), channel_id=1, source_target_pairs={{4,0},{5,1},{8,4},{9,5},{12,8},{13,9},{14,12},{15,13},{10,14},{11,... | collective-permute-start | bytes 1572872 | tf_op jit(solution)/shard_map/ppermute | solution.py:56
  (29 other events, 207.7 us)
where the time goes:
time: 173 us
  Pallas kernels  69.7 us (40%)
  waiting for transfers between devices  64.1 us (37%)
  starting transfers between devices  33.7 us (19%)
  other arithmetic  2.22 us (1%)
  local copies, waits for them, and re-layouts  2.1 us (1%)
    ppermute x21, waiting for transfers between devices, go(): self.held[step] = lax.ppermute(self.held[before], 'aux', way)  54.5 us
    pallas_call x8, Pallas kernels, gain(): pl.pallas_call(functools.partial(gain_kernel, places, not before), out_sh...  41.4 us
    ppermute x21, starting transfers between devices, go(): self.held[step] = lax.ppermute(self.held[before], 'aux', way)  23.1 us
    pallas_call x2, Pallas kernels, close(): pl.pallas_call(functools.partial(close_kernel, first, len(extra)), out_sh...  14.7 us
    ppermute x4, waiting for transfers between devices, fold_group(): theirs.append([lax.ppermute(mine[-1], 'tau', shift) for shift in shifts])  9.48 us
    pallas_call x2, Pallas kernels, pair_product(): pl.pallas_call(product_kernel, out_shape=jax.ShapeDtypeStruct((each, rows...  6.26 us
    ppermute x24, starting transfers between devices, swap(): self.pairs[step] = lax.ppermute(self.held[step], 'aux', self.cores)  5.32 us
    ppermute x4, starting transfers between devices, fold_group(): theirs.append([lax.ppermute(mine[-1], 'tau', shift) for shift in shifts])  5.27 us
  transfers between devices with their start and end apart: 49, of which 18 were waited for; matrix products, arithmetic and copies ran while one was open for 2% of the time, Pallas kernels for 32%

commit v1 on v0

--- a/solution.py
+++ b/solution.py
@@ -17,6 +17,7 @@
 
 def room(mib):
     return pltpu.CompilerParams(vmem_limit_bytes=mib * MIB)
+
 
 STRIP = 16
 
@@ -200,7 +201,7 @@
 
 
 def mix(folded, weights, order, sizes):
-    times, rows, width = folded[0][0].shape
+    _, rows, width = folded[0][0].shape
     parts = len(folded[0])
     panel = width * parts
     return pl.pallas_call(
@@ -214,35 +215,32 @@
     )(weights, order, *[f for g in folded for f in g])
 
 
-GAIN = 2
+LEAST = 3
+GAIN_ROOM, CLOSE_ROOM = 12, 18
 TOKEN = jax.ShapeDtypeStruct((8, 128), F32)
 
 
-def columns(ref, chip, wide):
+def columns(ref, owner, depth):
     if len(ref.shape) == 3:
-        return ref[chip]
-    return ref[:, pl.ds(pl.multiple_of(chip * wide, wide), wide)]
+        return ref[owner]
+    return ref[:, pl.ds(pl.multiple_of(owner * depth, depth), depth)]
 
 
 def gain_kernel(places, fresh, owners, coef, panel, *refs):
-    count = 2 * len(places)
+    count = len(places)
     pieces, refs = refs[:count], refs[count:]
     before, (chi, step, slots) = refs[: len(refs) - 3], refs[len(refs) - 3 :]
-    each, depth, size = pieces[0].shape
-    wide = 2 * depth
+    each, depth, _ = pieces[0].shape
 
     def one_frequency(w, carry):
-        slot = slots.at[w]
-        for j, place in enumerate(places):
-            even = lax.rem(owners[2 * place], 2) == 0
-            mine, theirs = pieces[2 * j][w], pieces[2 * j + 1][w]
-            slot[j * wide : j * wide + depth, :] = jnp.where(even, mine, theirs)
-            slot[j * wide + depth : (j + 1) * wide, :] = jnp.where(even, theirs, mine)
+        for j, piece in enumerate(pieces):
+            slots[w, j * depth : (j + 1) * depth, :] = piece[w]
         for left, out, old in ((panel, step, 1), (coef, chi, 0)):
             total = None if fresh else before[old][w]
-            for j, place in enumerate(places):
-                chip = owners[2 * place] // 2
-                term = dot(columns(left, chip, wide), slot[j * wide : (j + 1) * wide, :])
+            for j in range(0, count, 2):
+                block = [columns(left, owners[p], depth) for p in places[j : j + 2]]
+                right = slots[w, j * depth : (j + len(block)) * depth, :]
+                term = dot(jnp.concatenate(block, axis=1), right)
                 total = term if total is None else total + term
             out[w] = total
         return carry
@@ -261,9 +259,9 @@
         ],
         in_specs=[pl.BlockSpec(memory_space=pltpu.SMEM)] + [VMEM] * (2 + len(pieces) + len(before)),
         out_specs=[VMEM] * 2,
-        scratch_shapes=[pltpu.VMEM((each, 2 * depth * len(places), size), BF16)],
+        scratch_shapes=[pltpu.VMEM((each, depth * len(places), size), BF16)],
         input_output_aliases={3 + len(pieces) + i: i for i in range(len(before))},
-        compiler_params=room(20),
+        compiler_params=room(GAIN_ROOM),
         name="gain",
     )(owners, coef, panel, *pieces, *before)
 
@@ -271,7 +269,7 @@
 def close_kernel(first, aliased, column, chi, step, *refs):
     out, token, result, sems = refs[aliased:]
     token[...] = jnp.zeros_like(token)
-    each, rows, size = chi.shape
+    each, rows, _ = chi.shape
     cuts = sems.shape[1]
     part = rows // cuts
 
@@ -312,7 +310,7 @@
             pltpu.SemaphoreType.DMA((each, cuts)),
         ],
         input_output_aliases={} if before is None else {3: 0},
-        compiler_params=room(24),
+        compiler_params=room(CLOSE_ROOM),
         name="close",
     )(column, chi, step, *extra)
 
@@ -401,66 +399,85 @@
             moves = [m[lane][n] for m in (ups, downs) if n < len(m[lane])]
             plan.append(moves)
     count = len(plan)
-    points_of_chip = points // chips
+    share = points // size
     left = coefficients
-    if points_of_chip % 128:
-        left = jnp.swapaxes(left.reshape(rows, chips, points_of_chip), 0, 1)
-        panel[0] = jnp.swapaxes(panel[0].reshape(panel_size, chips, points_of_chip), 0, 1)
+    if share % 128:
+        left = jnp.swapaxes(left.reshape(rows, size, share), 0, 1)
+        panel[0] = jnp.swapaxes(panel[0].reshape(panel_size, size, share), 0, 1)
     sums, summed = {}, {c: 0 for c in range(len(rings))}
 
-    def add(c, steps):
+    def add(c, units):
         listed = ring_steps(chips, ways[c])
-        pieces = [p for s in steps for p in (rings[c].held[s], rings[c].pairs[s])]
-        places = tuple(listed.index(s) for s in steps)
-        chi, step = gain(
-            left, panel[0], pieces, early[ways[c]], places, sums.get(c, [])
+        pieces = [(rings[c].pairs if pair else rings[c].held)[s] for s, pair in units]
+        places = tuple(2 * listed.index(s) + pair for s, pair in units)
+        chi, step = gain(left, panel[0], pieces, early[ways[c]], places, sums.get(c, []))
+        sums[c] = [chi, step]
+        summed[c] += len(units)
+
+    def finish(c):
+        outs[0], mark = close(
+            panel[1], *sums[c], freqs, sum(sizes[:c]), outs[0], marks[-1] if marks else None
         )
-        sums[c] = [chi, step]
-        summed[c] += len(steps)
-        if summed[c] == chips:
-            outs[0], mark = close(
-                panel[1], chi, step, freqs, sum(sizes[:c]), outs[0], marks[-1] if marks else None
-            )
-            marks.append(mark)
-
-    waiting, swapped = {c: [] for c in range(len(rings))}, []
-
-    def add_waiting():
+        marks.append(mark)
+
+    waiting, swapped, closing = {c: [] for c in range(len(rings))}, [], []
+
+    def add_waiting(least):
         for c in range(len(rings)):
-            last = summed[c] + len(waiting[c]) == chips
-            while len(waiting[c]) >= GAIN or (last and waiting[c]):
-                add(c, waiting[c][:GAIN])
-                del waiting[c][:GAIN]
+            last = summed[c] + len(waiting[c]) == size
+            if waiting[c] and (last or len(waiting[c]) >= least):
+                add(c, waiting[c])
+                waiting[c] = []
 
     for number in range(count + 1):
         moves = plan[number] if number < count else []
         landed = plan[number - 1] if number else []
         sources = [(i, s - 1 if s > 0 else s + 1) for i, s in moves]
-        started = [(i, s) for i, s in dict.fromkeys(sources) if s == 0 and not rings[i].pairs]
+        started = [
+            (i, s) for i, s in dict.fromkeys(sources) if s == 0 and 0 not in rings[i].pairs
+        ]
         sync = [(rings[i].held, s) for i, s in dict.fromkeys(sources + landed)]
         sync += [(rings[i].pairs, s) for i, s in swapped]
         if number == 1:
             sync += [(panel, 0), (panel, 1)]
-        sync += [(sums[c], k) for c in sums for k in range(2) if summed[c] < chips]
-        if marks and summed[len(rings) - 1] < chips:
+        sync += [(sums[c], k) for c in sums for k in range(2) if summed[c] < size or c in closing]
+        if marks:
             sync += [(marks, len(marks) - 1)]
-        if number < count:
-            together(sync)
+        together(sync)
         for i, s in moves:
             rings[i].go(s)
+        now = list(dict.fromkeys(started + landed))
+        for i, s in now:
+            waiting[i].append((s, 0))
+        for i, s in swapped:
+            waiting[i].append((s, 1))
         before = dict(summed)
-        add_waiting()
-        now = list(dict.fromkeys(started + landed))
-        grown = [c for c in sums if before[c] < summed[c] < chips]
-        if grown and moves:
-            together([(rings[i].held, s) for i, s in now] + [(sums[c], k) for c in grown for k in range(2)])
-        for i, s in now:
-            rings[i].swap(s)
-            waiting[i].append(s)
+        due, closing = closing, []
+        if moves:
+            add_waiting(LEAST)
+            for c in due:
+                finish(c)
+            closing = [c for c in sums if before[c] < summed[c] == size]
+            grown = [c for c in sums if before[c] < summed[c]]
+            if grown and LATE_SWAPS:
+                together(
+                    [(rings[i].held, s) for i, s in now] + [(sums[c], k) for c in grown for k in range(2)]
+                )
+            for i, s in now:
+                rings[i].swap(s)
+        else:
+            for i, s in now:
+                rings[i].swap(s)
+            add_waiting(1)
+            for c in due:
+                finish(c)
         swapped = now
-        if number >= count - 1:
-            swapped = []
-            add_waiting()
+    for i, s in swapped:
+        waiting[i].append((s, 1))
+    add_waiting(1)
+    for c in range(len(rings)):
+        if c >= len(marks):
+            finish(c)
     return outs[0]
 
 
@@ -470,8 +487,12 @@
         box[key] = value
 
 
+LATE_SWAPS = False
+
+
 def solution(mesh):
     placed = (P("aux", None), P("tau", "aux", None), P("tau", "aux", None), P(), P())
+
     return jax.shard_map(
         per_device, mesh=mesh, in_specs=placed, out_specs=P("tau", "aux", None), check_vma=False
     )

time: 173 us -> 175 us (1.012)
  Pallas kernels: 69.7 us -> 76.7 us
  waiting for transfers between devices: 64.1 us -> 60.1 us
    pallas_call x8 -> x10, Pallas kernels: 41.4 us -> 48.4 us  [gain(): pl.pallas_call(functools.partial(gain_kernel, places, not before), out_sh...]
    ppermute x21, waiting for transfers between devices: 54.5 us -> 50.6 us  [go(): self.held[step] = lax.ppermute(self.held[before], 'aux', way)]
  transfers between devices with their start and end apart: 49 -> 49, of which waited for: 18 -> 19; matrix products, arithmetic and copies ran while one was open for 2% -> 2% of each run, Pallas kernels for 32% -> 36%
where the time goes in v1:
time: 175 us
  Pallas kernels  76.7 us (44%)
  waiting for transfers between devices  60.1 us (34%)
  starting transfers between devices  32.9 us (19%)
  other arithmetic  2.22 us (1%)
  local copies, waits for them, and re-layouts  2.1 us (1%)
    ppermute x21, waiting for transfers between devices, go(): self.held[step] = lax.ppermute(self.held[before], 'aux', way)  50.6 us
    pallas_call x10, Pallas kernels, gain(): pl.pallas_call(functools.partial(gain_kernel, places, not before), out_sh...  48.4 us
    ppermute x21, starting transfers between devices, go(): self.held[step] = lax.ppermute(self.held[before], 'aux', way)  23 us
    pallas_call x2, Pallas kernels, close(): pl.pallas_call(functools.partial(close_kernel, first, len(extra)), out_sh...  14.7 us
    ppermute x4, waiting for transfers between devices, fold_group(): theirs.append([lax.ppermute(mine[-1], 'tau', shift) for shift in shifts])  9.48 us
    pallas_call x2, Pallas kernels, pair_product(): pl.pallas_call(product_kernel, out_shape=jax.ShapeDtypeStruct((each, rows...  6.26 us
    ppermute x4, starting transfers between devices, fold_group(): theirs.append([lax.ppermute(mine[-1], 'tau', shift) for shift in shifts])  5.26 us
    pallas_call x4, Pallas kernels, fold(): pl.pallas_call(functools.partial(fold_kernel, len(products)), out_shape=j...  4.96 us
  transfers between devices with their start and end apart: 49, of which 19 were waited for; matrix products, arithmetic and copies ran while one was open for 2% of the time, Pallas kernels for 36%

profile of v1, /device:TPU:0, one launch (start us, length us, event | category | flops | bytes accessed | tf_op | source)
XLA Modules:
  0.0 175.1 jit_solution(4905055687749108635)
XLA Ops:
  1.5 3.0 %collective-permute-start.1 = (bf16[32,2048]{1,0:T(8,128)(2,1)S(1)}, bf16[32,2048]{1,0:T(8,128)(2,1)S(1)}, u32[]{:S(2)}, u32[]{:S(2)}) collective-permute-start(bf16[32,2048]{1,0:T(8,128)(2,1)S(1)} %bitcast.8), channel_id=1, source_target_pairs={{4,0},{5,1},{8,4},{9,5},{12,8},{13,9},{14,12},{15,13},{10,14},{11,... | collective-permute-start | bytes 393224 | tf_op jit(solution)/shard_map/ppermute | solution.py:57
  8.0 3.2 %product.2.refs_0_ = bf16[4,128,2048]{2,1,0:T(8,128)(2,1)S(1)} custom-call(bf16[8,128,2048]{2,1,0:T(8,128)(2,1)} %a.3, bf16[8,128,2048]{2,1,0:T(8,128)(2,1)} %b.3), custom_call_target="tpu_custom_call" | custom-call | tf_op jit(solution)/shard_map/product/pallas_call | solution.py:87
  13.8 3.1 %product.3.refs_1_ = bf16[4,128,2048]{2,1,0:T(8,128)(2,1)S(1)} custom-call(bf16[8,128,2048]{2,1,0:T(8,128)(2,1)} %a.3, bf16[8,128,2048]{2,1,0:T(8,128)(2,1)} %b.3), custom_call_target="tpu_custom_call" | custom-call | tf_op jit(solution)/shard_map/product/pallas_call | solution.py:87
  28.3 2.9 %collective-permute-done.14.refs_2_.refs_12_ = bf16[32,2048]{1,0:T(8,128)(2,1)S(1)} collective-permute-done((bf16[32,2048]{1,0:T(8,128)(2,1)S(1)}, bf16[32,2048]{1,0:T(8,128)(2,1)S(1)}, u32[]{:S(2)}, u32[]{:S(2)}) %collective-permute-start.14) | collective-permute-done | bytes 131104 | tf_op jit(solution)/shard_map/ppermute | solution.py:57
  37.6 4.6 %collective-permute-done.17.refs_6_ = bf16[8,128,128]{2,1,0:T(8,128)(2,1)S(1)} collective-permute-done((bf16[8,128,128]{2,1,0:T(8,128)(2,1)S(1)}, bf16[8,128,128]{2,1,0:T(8,128)(2,1)S(1)}, u32[]{:S(2)}, u32[]{:S(2)}) %collective-permute-start.17) | collective-permute-done | bytes 262176 | tf_op jit(solution)/shard_map/ppermute | solution.py:359
  42.2 4.7 %collective-permute-done.18.refs_7_ = bf16[8,128,128]{2,1,0:T(8,128)(2,1)S(1)} collective-permute-done((bf16[8,128,128]{2,1,0:T(8,128)(2,1)S(1)}, bf16[8,128,128]{2,1,0:T(8,128)(2,1)S(1)}, u32[]{:S(2)}, u32[]{:S(2)}) %collective-permute-start.18) | collective-permute-done | bytes 262176 | tf_op jit(solution)/shard_map/ppermute | solution.py:359
  51.4 11.5 %collective-permute-done.20.refs_2_ = bf16[4,128,512]{2,1,0:T(8,128)(2,1)S(1)} collective-permute-done((bf16[4,128,512]{2,1,0:T(8,128)(2,1)S(1)}, bf16[4,128,512]{2,1,0:T(8,128)(2,1)S(1)}, u32[]{:S(2)}, u32[]{:S(2)}) %collective-permute-start.20) | collective-permute-done | bytes 524320 | tf_op jit(solution)/shard_map/ppermute | solution.py:57
  65.6 4.5 %gain.10 = (f32[4,1024,512]{2,1,0:T(8,128)S(1)}, f32[4,512,512]{2,1,0:T(8,128)S(1)}) custom-call(s32[16]{0:T(128)S(1)} %get-tuple-element.125.owners, bf16[1024,2048]{1,0:T(8,128)(2,1)S(1)} %copy-done.2, bf16[512,2048]{1,0:T(8,128)(2,1)S(1)} %get-tuple-element.122.panel, bf16[4,128,512]{2,1,0:T(8,128)(2,1)S(1)} %get-tuple-element.116.refs_0_, ...), custom_call_target="tpu_custom_call" | custom-call | tf_op jit(solution)/shard_map/gain/pallas_call | solution.py:254
  70.1 7.6 %collective-permute-done.22.refs_0_ = bf16[4,128,512]{2,1,0:T(8,128)(2,1)S(1)} collective-permute-done((bf16[4,128,512]{2,1,0:T(8,128)(2,1)S(1)}, bf16[4,128,512]{2,1,0:T(8,128)(2,1)S(1)}, u32[]{:S(2)}, u32[]{:S(2)}) %collective-permute-start.22) | collective-permute-done | bytes 524320 | tf_op jit(solution)/shard_map/ppermute | solution.py:57
  81.2 5.4 %gain.11 = (f32[4,1024,512]{2,1,0:T(8,128)S(1)}, f32[4,512,512]{2,1,0:T(8,128)S(1)}) custom-call(s32[16]{0:T(128)S(1)} %get-tuple-element.125.owners, bf16[1024,2048]{1,0:T(8,128)(2,1)S(1)} %copy-done.2, bf16[512,2048]{1,0:T(8,128)(2,1)S(1)} %get-tuple-element.122.panel, ...), custom_call_target="tpu_custom_call", output_to_operand_aliasing={{0}: (7, {}), {1}: (8, {})} | custom-call | tf_op jit(solution)/shard_map/gain/pallas_call | solution.py:254
  86.6 6.7 %collective-permute-done.26.refs_0_ = bf16[4,128,512]{2,1,0:T(8,128)(2,1)S(1)} collective-permute-done((bf16[4,128,512]{2,1,0:T(8,128)(2,1)S(1)}, bf16[4,128,512]{2,1,0:T(8,128)(2,1)S(1)}, u32[]{:S(2)}, u32[]{:S(2)}) %collective-permute-start.26) | collective-permute-done | bytes 524320 | tf_op jit(solution)/shard_map/ppermute | solution.py:57
  97.4 5.4 %gain.12 = (f32[4,1024,512]{2,1,0:T(8,128)S(1)}, f32[4,512,512]{2,1,0:T(8,128)S(1)}) custom-call(s32[16]{0:T(128)S(1)} %get-tuple-element.125.owners, bf16[1024,2048]{1,0:T(8,128)(2,1)S(1)} %copy-done.2, bf16[512,2048]{1,0:T(8,128)(2,1)S(1)} %get-tuple-element.122.panel, ...), custom_call_target="tpu_custom_call", output_to_operand_aliasing={{0}: (7, {}), {1}: (8, {})} | custom-call | tf_op jit(solution)/shard_map/gain/pallas_call | solution.py:254
  102.8 6.4 %collective-permute-done.30.refs_1_ = bf16[4,128,512]{2,1,0:T(8,128)(2,1)S(1)} collective-permute-done((bf16[4,128,512]{2,1,0:T(8,128)(2,1)S(1)}, bf16[4,128,512]{2,1,0:T(8,128)(2,1)S(1)}, u32[]{:S(2)}, u32[]{:S(2)}) %collective-permute-start.30) | collective-permute-done | bytes 524320 | tf_op jit(solution)/shard_map/ppermute | solution.py:57
  112.7 4.4 %gain.14 = (f32[4,1024,512]{2,1,0:T(8,128)S(1)}, f32[4,512,512]{2,1,0:T(8,128)S(1)}) custom-call(s32[16]{0:T(128)S(1)} %get-tuple-element.121.owners, bf16[1024,2048]{1,0:T(8,128)(2,1)S(1)} %copy-done.2, bf16[512,2048]{1,0:T(8,128)(2,1)S(1)} %get-tuple-element.122.panel, bf16[4,128,512]{2,1,0:T(8,128)(2,1)S(1)} %get-tuple-element.147.refs_0_, ...), custom_call_target="tpu_custom_call" | custom-call | tf_op jit(solution)/shard_map/gain/pallas_call | solution.py:254
  117.2 5.3 %gain.13 = (f32[4,1024,512]{2,1,0:T(8,128)S(1)}, f32[4,512,512]{2,1,0:T(8,128)S(1)}) custom-call(s32[16]{0:T(128)S(1)} %get-tuple-element.125.owners, bf16[1024,2048]{1,0:T(8,128)(2,1)S(1)} %copy-done.2, bf16[512,2048]{1,0:T(8,128)(2,1)S(1)} %get-tuple-element.122.panel, ...), custom_call_target="tpu_custom_call", output_to_operand_aliasing={{0}: (6, {}), {1}: (7, {})} | custom-call | tf_op jit(solution)/shard_map/gain/pallas_call | solution.py:254
  123.7 2.4 %collective-permute-done.36.refs_1_ = bf16[4,128,512]{2,1,0:T(8,128)(2,1)S(1)} collective-permute-done((bf16[4,128,512]{2,1,0:T(8,128)(2,1)S(1)}, bf16[4,128,512]{2,1,0:T(8,128)(2,1)S(1)}, u32[]{:S(2)}, u32[]{:S(2)}) %collective-permute-start.36) | collective-permute-done | bytes 524320 | tf_op jit(solution)/shard_map/ppermute | solution.py:57
  128.3 3.6 %gain.15 = (f32[4,1024,512]{2,1,0:T(8,128)S(1)}, f32[4,512,512]{2,1,0:T(8,128)S(1)}) custom-call(s32[16]{0:T(128)S(1)} %get-tuple-element.125.owners, bf16[1024,2048]{1,0:T(8,128)(2,1)S(1)} %copy-done.2, bf16[512,2048]{1,0:T(8,128)(2,1)S(1)} %get-tuple-element.122.panel, ...), custom_call_target="tpu_custom_call", output_to_operand_aliasing={{0}: (4, {}), {1}: (5, {})} | custom-call | tf_op jit(solution)/shard_map/gain/pallas_call | solution.py:254
  131.9 5.3 %gain.16 = (f32[4,1024,512]{2,1,0:T(8,128)S(1)}, f32[4,512,512]{2,1,0:T(8,128)S(1)}) custom-call(s32[16]{0:T(128)S(1)} %get-tuple-element.121.owners, bf16[1024,2048]{1,0:T(8,128)(2,1)S(1)} %copy-done.2, bf16[512,2048]{1,0:T(8,128)(2,1)S(1)} %get-tuple-element.122.panel, ...), custom_call_target="tpu_custom_call", output_to_operand_aliasing={{0}: (6, {}), {1}: (7, {})} | custom-call | tf_op jit(solution)/shard_map/gain/pallas_call | solution.py:254
  137.3 3.2 %collective-permute-done.39.refs_0_ = bf16[4,128,512]{2,1,0:T(8,128)(2,1)S(1)} collective-permute-done((bf16[4,128,512]{2,1,0:T(8,128)(2,1)S(1)}, bf16[4,128,512]{2,1,0:T(8,128)(2,1)S(1)}, u32[]{:S(2)}, u32[]{:S(2)}) %collective-permute-start.39) | collective-permute-done | bytes 524320 | tf_op jit(solution)/shard_map/ppermute | solution.py:57
  144.2 7.1 %close.2 = (f32[8,1024,512]{2,1,0:T(8,128)}, f32[8,128]{1,0:T(8,128)S(1)}) custom-call(f32[512,1]{1,0:T(8,128)S(1)} %get-tuple-element.120.column, f32[4,1024,512]{2,1,0:T(8,128)S(1)} %get-tuple-element.179.chi, f32[4,512,512]{2,1,0:T(8,128)S(1)} %get-tuple-element.180.step), custom_call_target="tpu_custom_call" | custom-call | tf_op jit(solution)/shard_map/close/pallas_call | solution.py:303
  151.3 5.4 %gain.17 = (f32[4,1024,512]{2,1,0:T(8,128)S(1)}, f32[4,512,512]{2,1,0:T(8,128)S(1)}) custom-call(s32[16]{0:T(128)S(1)} %get-tuple-element.121.owners, bf16[1024,2048]{1,0:T(8,128)(2,1)S(1)} %copy-done.2, bf16[512,2048]{1,0:T(8,128)(2,1)S(1)} %get-tuple-element.122.panel, ...), custom_call_target="tpu_custom_call", output_to_operand_aliasing={{0}: (7, {}), {1}: (8, {})} | custom-call | tf_op jit(solution)/shard_map/gain/pallas_call | solution.py:254
  158.1 5.4 %gain.18 = (f32[4,1024,512]{2,1,0:T(8,128)S(1)}, f32[4,512,512]{2,1,0:T(8,128)S(1)}) custom-call(s32[16]{0:T(128)S(1)} %get-tuple-element.121.owners, bf16[1024,2048]{1,0:T(8,128)(2,1)S(1)} %copy-done.2, bf16[512,2048]{1,0:T(8,128)(2,1)S(1)} %get-tuple-element.122.panel, ...), custom_call_target="tpu_custom_call", output_to_operand_aliasing={{0}: (7, {}), {1}: (8, {})} | custom-call | tf_op jit(solution)/shard_map/gain/pallas_call | solution.py:254
  163.5 3.7 %gain.19 = (f32[4,1024,512]{2,1,0:T(8,128)S(1)}, f32[4,512,512]{2,1,0:T(8,128)S(1)}) custom-call(s32[16]{0:T(128)S(1)} %get-tuple-element.121.owners, bf16[1024,2048]{1,0:T(8,128)(2,1)S(1)} %copy-done.2, bf16[512,2048]{1,0:T(8,128)(2,1)S(1)} %get-tuple-element.122.panel, ...), custom_call_target="tpu_custom_call", output_to_operand_aliasing={{0}: (5, {}), {1}: (6, {})} | custom-call | tf_op jit(solution)/shard_map/gain/pallas_call | solution.py:254
  167.3 7.6 %close.3 = (f32[8,1024,512]{2,1,0:T(8,128)}, f32[8,128]{1,0:T(8,128)}) custom-call(f32[512,1]{1,0:T(8,128)S(1)} %get-tuple-element.120.column, f32[4,1024,512]{2,1,0:T(8,128)S(1)} %get-tuple-element.190.chi, f32[4,512,512]{2,1,0:T(8,128)S(1)} %get-tuple-element.191.step, ...), custom_call_target="tpu_custom_call", output_to_operand_aliasing={{0}: (3, {})} | custom-call | tf_op jit(solution)/shard_map/close/pallas_call | solution.py:303
  (125 shorter events, 52.2 us)
Async XLA Ops:
  36.0 10.8 %collective-permute-start.18 = (bf16[8,128,128]{2,1,0:T(8,128)(2,1)S(1)}, bf16[8,128,128]{2,1,0:T(8,128)(2,1)S(1)}, u32[]{:S(2)}, u32[]{:S(2)}) collective-permute-start(bf16[8,128,128]{2,1,0:T(8,128)(2,1)S(1)} %fold.7.refs_3_), channel_id=1, source_target_pairs={{16,0},{0,16},{17,1},{1,17},{18,2},{2,18},{19,3},{3,19},{20,4},{4,... | collective-permute-start | bytes 786440 | tf_op jit(solution)/shard_map/ppermute | solution.py:359
  48.5 14.3 %collective-permute-start.20 = (bf16[4,128,512]{2,1,0:T(8,128)(2,1)S(1)}, bf16[4,128,512]{2,1,0:T(8,128)(2,1)S(1)}, u32[]{:S(2)}, u32[]{:S(2)}) collective-permute-start(bf16[4,128,512]{2,1,0:T(8,128)(2,1)S(1)} %get-tuple-element.116.refs_0_), channel_id=1, source_target_pairs={{4,0},{5,1},{8,4},{9,5},{12,8},{13,9},{14,12},{15,13},{10,14},{11,... | collective-permute-start | bytes 1572872 | tf_op jit(solution)/shard_map/ppermute | solution.py:57
  49.3 14.0 %collective-permute-start.19 = (bf16[4,128,512]{2,1,0:T(8,128)(2,1)S(1)}, bf16[4,128,512]{2,1,0:T(8,128)(2,1)S(1)}, u32[]{:S(2)}, u32[]{:S(2)}) collective-permute-start(bf16[4,128,512]{2,1,0:T(8,128)(2,1)S(1)} %get-tuple-element.116.refs_0_), channel_id=1, source_target_pairs={{0,4},{1,5},{4,8},{5,9},{8,12},{9,13},{12,14},{13,15},{14,10},{15,... | collective-permute-start | bytes 1572872 | tf_op jit(solution)/shard_map/ppermute | solution.py:57
  63.3 14.3 %collective-permute-start.22 = (bf16[4,128,512]{2,1,0:T(8,128)(2,1)S(1)}, bf16[4,128,512]{2,1,0:T(8,128)(2,1)S(1)}, u32[]{:S(2)}, u32[]{:S(2)}) collective-permute-start(bf16[4,128,512]{2,1,0:T(8,128)(2,1)S(1)} %collective-permute-done.19.refs_1_), channel_id=1, source_target_pairs={{0,4},{1,5},{4,8},{5,9},{8,12},{9,13},{12,14},{13,15},{14,10},{15,... | collective-permute-start | bytes 1572872 | tf_op jit(solution)/shard_map/ppermute | solution.py:57
  64.6 13.0 %collective-permute-start.25 = (bf16[4,128,512]{2,1,0:T(8,128)(2,1)S(1)}, bf16[4,128,512]{2,1,0:T(8,128)(2,1)S(1)}, u32[]{:S(2)}, u32[]{:S(2)}) collective-permute-start(bf16[4,128,512]{2,1,0:T(8,128)(2,1)S(1)} %collective-permute-done.20.refs_2_), channel_id=1, source_target_pairs={{0,1},{1,0},{2,3},{3,2},{4,5},{5,4},{6,7},{7,6},{8,9},{9,8},{10,11... | collective-permute-start | bytes 1572872 | tf_op jit(solution)/shard_map/ppermute | solution.py:52
  64.8 14.1 %collective-permute-start.23 = (bf16[4,128,512]{2,1,0:T(8,128)(2,1)S(1)}, bf16[4,128,512]{2,1,0:T(8,128)(2,1)S(1)}, u32[]{:S(2)}, u32[]{:S(2)}) collective-permute-start(bf16[4,128,512]{2,1,0:T(8,128)(2,1)S(1)} %collective-permute-done.20.refs_2_), channel_id=1, source_target_pairs={{4,0},{5,1},{8,4},{9,5},{12,8},{13,9},{14,12},{15,13},{10,14},{11,... | collective-permute-start | bytes 1572872 | tf_op jit(solution)/shard_map/ppermute | solution.py:57
  79.0 14.3 %collective-permute-start.26 = (bf16[4,128,512]{2,1,0:T(8,128)(2,1)S(1)}, bf16[4,128,512]{2,1,0:T(8,128)(2,1)S(1)}, u32[]{:S(2)}, u32[]{:S(2)}) collective-permute-start(bf16[4,128,512]{2,1,0:T(8,128)(2,1)S(1)} %collective-permute-done.22.refs_0_), channel_id=1, source_target_pairs={{0,4},{1,5},{4,8},{5,9},{8,12},{9,13},{12,14},{13,15},{14,10},{15,... | collective-permute-start | bytes 1572872 | tf_op jit(solution)/shard_map/ppermute | solution.py:57
  80.5 12.8 %collective-permute-start.29 = (bf16[4,128,512]{2,1,0:T(8,128)(2,1)S(1)}, bf16[4,128,512]{2,1,0:T(8,128)(2,1)S(1)}, u32[]{:S(2)}, u32[]{:S(2)}) collective-permute-start(bf16[4,128,512]{2,1,0:T(8,128)(2,1)S(1)} %collective-permute-done.23.refs_1_), channel_id=1, source_target_pairs={{0,1},{1,0},{2,3},{3,2},{4,5},{5,4},{6,7},{7,6},{8,9},{9,8},{10,11... | collective-permute-start | bytes 1572872 | tf_op jit(solution)/shard_map/ppermute | solution.py:52
  80.8 14.1 %collective-permute-start.27 = (bf16[4,128,512]{2,1,0:T(8,128)(2,1)S(1)}, bf16[4,128,512]{2,1,0:T(8,128)(2,1)S(1)}, u32[]{:S(2)}, u32[]{:S(2)}) collective-permute-start(bf16[4,128,512]{2,1,0:T(8,128)(2,1)S(1)} %collective-permute-done.23.refs_1_), channel_id=1, source_target_pairs={{4,0},{5,1},{8,4},{9,5},{12,8},{13,9},{14,12},{15,13},{10,14},{11,... | collective-permute-start | bytes 1572872 | tf_op jit(solution)/shard_map/ppermute | solution.py:57
  95.4 13.8 %collective-permute-start.30 = (bf16[4,128,512]{2,1,0:T(8,128)(2,1)S(1)}, bf16[4,128,512]{2,1,0:T(8,128)(2,1)S(1)}, u32[]{:S(2)}, u32[]{:S(2)}) collective-permute-start(bf16[4,128,512]{2,1,0:T(8,128)(2,1)S(1)} %get-tuple-element.147.refs_0_), channel_id=1, source_target_pairs={{4,0},{5,1},{8,4},{9,5},{12,8},{13,9},{14,12},{15,13},{10,14},{11,... | collective-permute-start | bytes 1572872 | tf_op jit(solution)/shard_map/ppermute | solution.py:57
  95.8 13.4 %collective-permute-start.33 = (bf16[4,128,512]{2,1,0:T(8,128)(2,1)S(1)}, bf16[4,128,512]{2,1,0:T(8,128)(2,1)S(1)}, u32[]{:S(2)}, u32[]{:S(2)}) collective-permute-start(bf16[4,128,512]{2,1,0:T(8,128)(2,1)S(1)} %collective-permute-done.26.refs_0_), channel_id=1, source_target_pairs={{0,1},{1,0},{2,3},{3,2},{4,5},{5,4},{6,7},{7,6},{8,9},{9,8},{10,11... | collective-permute-start | bytes 1572872 | tf_op jit(solution)/shard_map/ppermute | solution.py:52
  95.8 14.3 %collective-permute-start.31 = (bf16[4,128,512]{2,1,0:T(8,128)(2,1)S(1)}, bf16[4,128,512]{2,1,0:T(8,128)(2,1)S(1)}, u32[]{:S(2)}, u32[]{:S(2)}) collective-permute-start(bf16[4,128,512]{2,1,0:T(8,128)(2,1)S(1)} %collective-permute-done.26.refs_0_), channel_id=1, source_target_pairs={{0,4},{1,5},{4,8},{5,9},{8,12},{9,13},{12,14},{13,15},{14,10},{15,... | collective-permute-start | bytes 1572872 | tf_op jit(solution)/shard_map/ppermute | solution.py:57
  110.2 13.5 %collective-permute-start.35 = (bf16[4,128,512]{2,1,0:T(8,128)(2,1)S(1)}, bf16[4,128,512]{2,1,0:T(8,128)(2,1)S(1)}, u32[]{:S(2)}, u32[]{:S(2)}) collective-permute-start(bf16[4,128,512]{2,1,0:T(8,128)(2,1)S(1)} %get-tuple-element.147.refs_0_), channel_id=1, source_target_pairs={{0,4},{1,5},{4,8},{5,9},{8,12},{9,13},{12,14},{13,15},{14,10},{15,... | collective-permute-start | bytes 1572872 | tf_op jit(solution)/shard_map/ppermute | solution.py:57
  111.7 11.9 %collective-permute-start.37 = (bf16[4,128,512]{2,1,0:T(8,128)(2,1)S(1)}, bf16[4,128,512]{2,1,0:T(8,128)(2,1)S(1)}, u32[]{:S(2)}, u32[]{:S(2)}) collective-permute-start(bf16[4,128,512]{2,1,0:T(8,128)(2,1)S(1)} %collective-permute-done.31.refs_0_), channel_id=1, source_target_pairs={{0,1},{1,0},{2,3},{3,2},{4,5},{5,4},{6,7},{7,6},{8,9},{9,8},{10,11... | collective-permute-start | bytes 1572872 | tf_op jit(solution)/shard_map/ppermute | solution.py:52
  111.7 11.9 %collective-permute-start.38 = (bf16[4,128,512]{2,1,0:T(8,128)(2,1)S(1)}, bf16[4,128,512]{2,1,0:T(8,128)(2,1)S(1)}, u32[]{:S(2)}, u32[]{:S(2)}) collective-permute-start(bf16[4,128,512]{2,1,0:T(8,128)(2,1)S(1)} %collective-permute-done.30.refs_1_), channel_id=1, source_target_pairs={{0,1},{1,0},{2,3},{3,2},{4,5},{5,4},{6,7},{7,6},{8,9},{9,8},{10,11... | collective-permute-start | bytes 1572872 | tf_op jit(solution)/shard_map/ppermute | solution.py:52
  112.3 13.8 %collective-permute-start.36 = (bf16[4,128,512]{2,1,0:T(8,128)(2,1)S(1)}, bf16[4,128,512]{2,1,0:T(8,128)(2,1)S(1)}, u32[]{:S(2)}, u32[]{:S(2)}) collective-permute-start(bf16[4,128,512]{2,1,0:T(8,128)(2,1)S(1)} %collective-permute-done.30.refs_1_), channel_id=1, source_target_pairs={{4,0},{5,1},{8,4},{9,5},{12,8},{13,9},{14,12},{15,13},{10,14},{11,... | collective-permute-start | bytes 1572872 | tf_op jit(solution)/shard_map/ppermute | solution.py:57
  126.1 11.2 %collective-permute-start.41 = (bf16[4,128,512]{2,1,0:T(8,128)(2,1)S(1)}, bf16[4,128,512]{2,1,0:T(8,128)(2,1)S(1)}, u32[]{:S(2)}, u32[]{:S(2)}) collective-permute-start(bf16[4,128,512]{2,1,0:T(8,128)(2,1)S(1)} %collective-permute-done.35.refs_0_), channel_id=1, source_target_pairs={{0,1},{1,0},{2,3},{3,2},{4,5},{5,4},{6,7},{7,6},{8,9},{9,8},{10,11... | collective-permute-start | bytes 1572872 | tf_op jit(solution)/shard_map/ppermute | solution.py:52
  126.1 14.3 %collective-permute-start.39 = (bf16[4,128,512]{2,1,0:T(8,128)(2,1)S(1)}, bf16[4,128,512]{2,1,0:T(8,128)(2,1)S(1)}, u32[]{:S(2)}, u32[]{:S(2)}) collective-permute-start(bf16[4,128,512]{2,1,0:T(8,128)(2,1)S(1)} %collective-permute-done.35.refs_0_), channel_id=1, source_target_pairs={{0,4},{1,5},{4,8},{5,9},{8,12},{9,13},{12,14},{13,15},{14,10},{15,... | collective-permute-start | bytes 1572872 | tf_op jit(solution)/shard_map/ppermute | solution.py:57
  127.6 12.8 %collective-permute-start.42 = (bf16[4,128,512]{2,1,0:T(8,128)(2,1)S(1)}, bf16[4,128,512]{2,1,0:T(8,128)(2,1)S(1)}, u32[]{:S(2)}, u32[]{:S(2)}) collective-permute-start(bf16[4,128,512]{2,1,0:T(8,128)(2,1)S(1)} %collective-permute-done.36.refs_1_), channel_id=1, source_target_pairs={{0,1},{1,0},{2,3},{3,2},{4,5},{5,4},{6,7},{7,6},{8,9},{9,8},{10,11... | collective-permute-start | bytes 1572872 | tf_op jit(solution)/shard_map/ppermute | solution.py:52
  127.8 14.1 %collective-permute-start.40 = (bf16[4,128,512]{2,1,0:T(8,128)(2,1)S(1)}, bf16[4,128,512]{2,1,0:T(8,128)(2,1)S(1)}, u32[]{:S(2)}, u32[]{:S(2)}) collective-permute-start(bf16[4,128,512]{2,1,0:T(8,128)(2,1)S(1)} %collective-permute-done.36.refs_1_), channel_id=1, source_target_pairs={{4,0},{5,1},{8,4},{9,5},{12,8},{13,9},{14,12},{15,13},{10,14},{11,... | collective-permute-start | bytes 1572872 | tf_op jit(solution)/shard_map/ppermute | solution.py:57
  141.9 14.7 %collective-permute-start.45 = (bf16[4,128,512]{2,1,0:T(8,128)(2,1)S(1)}, bf16[4,128,512]{2,1,0:T(8,128)(2,1)S(1)}, u32[]{:S(2)}, u32[]{:S(2)}) collective-permute-start(bf16[4,128,512]{2,1,0:T(8,128)(2,1)S(1)} %collective-permute-done.39.refs_0_), channel_id=1, source_target_pairs={{0,1},{1,0},{2,3},{3,2},{4,5},{5,4},{6,7},{7,6},{8,9},{9,8},{10,11... | collective-permute-start | bytes 1572872 | tf_op jit(solution)/shard_map/ppermute | solution.py:52
  141.9 14.8 %collective-permute-start.43 = (bf16[4,128,512]{2,1,0:T(8,128)(2,1)S(1)}, bf16[4,128,512]{2,1,0:T(8,128)(2,1)S(1)}, u32[]{:S(2)}, u32[]{:S(2)}) collective-permute-start(bf16[4,128,512]{2,1,0:T(8,128)(2,1)S(1)} %collective-permute-done.39.refs_0_), channel_id=1, source_target_pairs={{0,4},{1,5},{4,8},{5,9},{8,12},{9,13},{12,14},{13,15},{14,10},{15,... | collective-permute-start | bytes 1572872 | tf_op jit(solution)/shard_map/ppermute | solution.py:57
  143.3 13.4 %collective-permute-start.46 = (bf16[4,128,512]{2,1,0:T(8,128)(2,1)S(1)}, bf16[4,128,512]{2,1,0:T(8,128)(2,1)S(1)}, u32[]{:S(2)}, u32[]{:S(2)}) collective-permute-start(bf16[4,128,512]{2,1,0:T(8,128)(2,1)S(1)} %collective-permute-done.40.refs_1_), channel_id=1, source_target_pairs={{0,1},{1,0},{2,3},{3,2},{4,5},{5,4},{6,7},{7,6},{8,9},{9,8},{10,11... | collective-permute-start | bytes 1572872 | tf_op jit(solution)/shard_map/ppermute | solution.py:52
  143.5 14.1 %collective-permute-start.44 = (bf16[4,128,512]{2,1,0:T(8,128)(2,1)S(1)}, bf16[4,128,512]{2,1,0:T(8,128)(2,1)S(1)}, u32[]{:S(2)}, u32[]{:S(2)}) collective-permute-start(bf16[4,128,512]{2,1,0:T(8,128)(2,1)S(1)} %collective-permute-done.40.refs_1_), channel_id=1, source_target_pairs={{4,0},{5,1},{8,4},{9,5},{12,8},{13,9},{14,12},{15,13},{10,14},{11,... | collective-permute-start | bytes 1572872 | tf_op jit(solution)/shard_map/ppermute | solution.py:57
  (29 other events, 218.0 us)

commit v2 on v1

--- a/solution.py
+++ b/solution.py
@@ -216,7 +216,7 @@
 
 
 LEAST = 3
-GAIN_ROOM, CLOSE_ROOM = 12, 18
+GAIN_ROOM, CLOSE_ROOM = 10, 16
 TOKEN = jax.ShapeDtypeStruct((8, 128), F32)
 
 
@@ -299,7 +299,7 @@
 def close(column, chi, step, total, first, before, mark):
     each, rows, size = chi.shape
     extra = [] if before is None else [before, mark]
-    cuts = 4
+    cuts = 8
     return pl.pallas_call(
         functools.partial(close_kernel, first, len(extra)),
         out_shape=[jax.ShapeDtypeStruct((total, rows, size), F32), TOKEN],
@@ -420,14 +420,15 @@
         )
         marks.append(mark)
 
-    waiting, swapped, closing = {c: [] for c in range(len(rings))}, [], []
+    waiting, swapped = {c: [] for c in range(len(rings))}, []
 
     def add_waiting(least):
-        for c in range(len(rings)):
-            last = summed[c] + len(waiting[c]) == size
-            if waiting[c] and (last or len(waiting[c]) >= least):
+        ends = [c for c in waiting if waiting[c] and summed[c] + len(waiting[c]) == size]
+        for c in ends if ends and least > 1 else range(len(rings)):
+            if waiting[c] and (c in ends or len(waiting[c]) >= least):
                 add(c, waiting[c])
                 waiting[c] = []
+        return ends if least > 1 else []
 
     for number in range(count + 1):
         moves = plan[number] if number < count else []
@@ -440,7 +441,7 @@
         sync += [(rings[i].pairs, s) for i, s in swapped]
         if number == 1:
             sync += [(panel, 0), (panel, 1)]
-        sync += [(sums[c], k) for c in sums for k in range(2) if summed[c] < size or c in closing]
+        sync += [(sums[c], k) for c in sums for k in range(2) if summed[c] < size]
         if marks:
             sync += [(marks, len(marks) - 1)]
         together(sync)
@@ -452,12 +453,9 @@
         for i, s in swapped:
             waiting[i].append((s, 1))
         before = dict(summed)
-        due, closing = closing, []
         if moves:
-            add_waiting(LEAST)
-            for c in due:
+            for c in add_waiting(LEAST):
                 finish(c)
-            closing = [c for c in sums if before[c] < summed[c] == size]
             grown = [c for c in sums if before[c] < summed[c]]
             if grown and LATE_SWAPS:
                 together(
@@ -469,8 +467,6 @@
             for i, s in now:
                 rings[i].swap(s)
             add_waiting(1)
-            for c in due:
-                finish(c)
         swapped = now
     for i, s in swapped:
         waiting[i].append((s, 1))

time: 175 us -> 176 us (level)
  waiting for transfers between devices: 60.1 us -> 62.1 us
    pallas_call x10 -> x9, Pallas kernels: 48.4 us -> 46.2 us  [gain(): pl.pallas_call(functools.partial(gain_kernel, places, not before), out_sh...]
    ppermute x21, waiting for transfers between devices: 50.6 us -> 52.5 us  [go(): self.held[step] = lax.ppermute(self.held[before], 'aux', way)]
  transfers between devices with their start and end apart: 49 -> 49, of which waited for: 19 -> 20; matrix products, arithmetic and copies ran while one was open for 2% -> 2% of each run, Pallas kernels for 36% -> 35%
where the time goes in v2:
time: 176 us; the launch traced here: 175 us
  Pallas kernels  75.1 us (43%)
  waiting for transfers between devices  62.1 us (35%)
  starting transfers between devices  32.9 us (19%)
  other arithmetic  2.22 us (1%)
  local copies, waits for them, and re-layouts  2.1 us (1%)
    ppermute x21, waiting for transfers between devices, go(): self.held[step] = lax.ppermute(self.held[before], 'aux', way)  52.5 us
    pallas_call x9, Pallas kernels, gain(): pl.pallas_call(functools.partial(gain_kernel, places, not before), out_sh...  46.2 us
    ppermute x21, starting transfers between devices, go(): self.held[step] = lax.ppermute(self.held[before], 'aux', way)  23 us
    pallas_call x2, Pallas kernels, close(): pl.pallas_call(functools.partial(close_kernel, first, len(extra)), out_sh...  15.3 us
    ppermute x4, waiting for transfers between devices, fold_group(): theirs.append([lax.ppermute(mine[-1], 'tau', shift) for shift in shifts])  9.48 us
    pallas_call x2, Pallas kernels, pair_product(): pl.pallas_call(product_kernel, out_shape=jax.ShapeDtypeStruct((each, rows...  6.26 us
    ppermute x4, starting transfers between devices, fold_group(): theirs.append([lax.ppermute(mine[-1], 'tau', shift) for shift in shifts])  5.27 us
    pallas_call x4, Pallas kernels, fold(): pl.pallas_call(functools.partial(fold_kernel, len(products)), out_shape=j...  4.96 us
  transfers between devices with their start and end apart: 49, of which 20 were waited for; matrix products, arithmetic and copies ran while one was open for 2% of the time, Pallas kernels for 35%

profile of v2, /device:TPU:0, one launch (start us, length us, event | category | flops | bytes accessed | tf_op | source)
XLA Modules:
  0.0 175.4 jit_solution(5108276676433674963)
XLA Ops:
  1.5 3.0 %collective-permute-start.1 = (bf16[32,2048]{1,0:T(8,128)(2,1)S(1)}, bf16[32,2048]{1,0:T(8,128)(2,1)S(1)}, u32[]{:S(2)}, u32[]{:S(2)}) collective-permute-start(bf16[32,2048]{1,0:T(8,128)(2,1)S(1)} %bitcast.8), channel_id=1, source_target_pairs={{4,0},{5,1},{8,4},{9,5},{12,8},{13,9},{14,12},{15,13},{10,14},{11,... | collective-permute-start | bytes 393224 | tf_op jit(solution)/shard_map/ppermute | solution.py:57
  8.0 3.2 %product.2.refs_0_ = bf16[4,128,2048]{2,1,0:T(8,128)(2,1)S(1)} custom-call(bf16[8,128,2048]{2,1,0:T(8,128)(2,1)} %a.3, bf16[8,128,2048]{2,1,0:T(8,128)(2,1)} %b.3), custom_call_target="tpu_custom_call" | custom-call | tf_op jit(solution)/shard_map/product/pallas_call | solution.py:87
  11.8 2.0 %collective-permute-start.2 = (bf16[32,2048]{1,0:T(8,128)(2,1)S(1)}, bf16[32,2048]{1,0:T(8,128)(2,1)S(1)}, u32[]{:S(2)}, u32[]{:S(2)}) collective-permute-start(bf16[32,2048]{1,0:T(8,128)(2,1)S(1)} %collective-permute-done.refs_2_.refs_0_), channel_id=1, source_target_pairs={{0,4},{1,5},{4,8},{5,9},{8,12},{9,13},{12,14},{13,15},{14,10},{15,... | collective-permute-start | bytes 393224 | tf_op jit(solution)/shard_map/ppermute | solution.py:57
  13.8 3.1 %product.3.refs_1_ = bf16[4,128,2048]{2,1,0:T(8,128)(2,1)S(1)} custom-call(bf16[8,128,2048]{2,1,0:T(8,128)(2,1)} %a.3, bf16[8,128,2048]{2,1,0:T(8,128)(2,1)} %b.3), custom_call_target="tpu_custom_call" | custom-call | tf_op jit(solution)/shard_map/product/pallas_call | solution.py:87
  28.3 2.9 %collective-permute-done.14.refs_2_.refs_12_ = bf16[32,2048]{1,0:T(8,128)(2,1)S(1)} collective-permute-done((bf16[32,2048]{1,0:T(8,128)(2,1)S(1)}, bf16[32,2048]{1,0:T(8,128)(2,1)S(1)}, u32[]{:S(2)}, u32[]{:S(2)}) %collective-permute-start.14) | collective-permute-done | bytes 131104 | tf_op jit(solution)/shard_map/ppermute | solution.py:57
  37.6 4.6 %collective-permute-done.17.refs_6_ = bf16[8,128,128]{2,1,0:T(8,128)(2,1)S(1)} collective-permute-done((bf16[8,128,128]{2,1,0:T(8,128)(2,1)S(1)}, bf16[8,128,128]{2,1,0:T(8,128)(2,1)S(1)}, u32[]{:S(2)}, u32[]{:S(2)}) %collective-permute-start.17) | collective-permute-done | bytes 262176 | tf_op jit(solution)/shard_map/ppermute | solution.py:359
  42.2 4.7 %collective-permute-done.18.refs_7_ = bf16[8,128,128]{2,1,0:T(8,128)(2,1)S(1)} collective-permute-done((bf16[8,128,128]{2,1,0:T(8,128)(2,1)S(1)}, bf16[8,128,128]{2,1,0:T(8,128)(2,1)S(1)}, u32[]{:S(2)}, u32[]{:S(2)}) %collective-permute-start.18) | collective-permute-done | bytes 262176 | tf_op jit(solution)/shard_map/ppermute | solution.py:359
  51.4 11.5 %collective-permute-done.20.refs_2_ = bf16[4,128,512]{2,1,0:T(8,128)(2,1)S(1)} collective-permute-done((bf16[4,128,512]{2,1,0:T(8,128)(2,1)S(1)}, bf16[4,128,512]{2,1,0:T(8,128)(2,1)S(1)}, u32[]{:S(2)}, u32[]{:S(2)}) %collective-permute-start.20) | collective-permute-done | bytes 524320 | tf_op jit(solution)/shard_map/ppermute | solution.py:57
  65.6 4.5 %gain.9 = (f32[4,1024,512]{2,1,0:T(8,128)S(1)}, f32[4,512,512]{2,1,0:T(8,128)S(1)}) custom-call(s32[16]{0:T(128)S(1)} %get-tuple-element.122.owners, bf16[1024,2048]{1,0:T(8,128)(2,1)S(1)} %copy-done.2, bf16[512,2048]{1,0:T(8,128)(2,1)S(1)} %get-tuple-element.119.panel, bf16[4,128,512]{2,1,0:T(8,128)(2,1)S(1)} %get-tuple-element.113.refs_0_, ...), custom_call_target="tpu_custom_call" | custom-call | tf_op jit(solution)/shard_map/gain/pallas_call | solution.py:254
  70.1 7.6 %collective-permute-done.22.refs_0_ = bf16[4,128,512]{2,1,0:T(8,128)(2,1)S(1)} collective-permute-done((bf16[4,128,512]{2,1,0:T(8,128)(2,1)S(1)}, bf16[4,128,512]{2,1,0:T(8,128)(2,1)S(1)}, u32[]{:S(2)}, u32[]{:S(2)}) %collective-permute-start.22) | collective-permute-done | bytes 524320 | tf_op jit(solution)/shard_map/ppermute | solution.py:57
  81.2 5.4 %gain.10 = (f32[4,1024,512]{2,1,0:T(8,128)S(1)}, f32[4,512,512]{2,1,0:T(8,128)S(1)}) custom-call(s32[16]{0:T(128)S(1)} %get-tuple-element.122.owners, bf16[1024,2048]{1,0:T(8,128)(2,1)S(1)} %copy-done.2, bf16[512,2048]{1,0:T(8,128)(2,1)S(1)} %get-tuple-element.119.panel, ...), custom_call_target="tpu_custom_call", output_to_operand_aliasing={{0}: (7, {}), {1}: (8, {})} | custom-call | tf_op jit(solution)/shard_map/gain/pallas_call | solution.py:254
  86.6 6.7 %collective-permute-done.26.refs_0_ = bf16[4,128,512]{2,1,0:T(8,128)(2,1)S(1)} collective-permute-done((bf16[4,128,512]{2,1,0:T(8,128)(2,1)S(1)}, bf16[4,128,512]{2,1,0:T(8,128)(2,1)S(1)}, u32[]{:S(2)}, u32[]{:S(2)}) %collective-permute-start.26) | collective-permute-done | bytes 524320 | tf_op jit(solution)/shard_map/ppermute | solution.py:57
  97.4 5.4 %gain.11 = (f32[4,1024,512]{2,1,0:T(8,128)S(1)}, f32[4,512,512]{2,1,0:T(8,128)S(1)}) custom-call(s32[16]{0:T(128)S(1)} %get-tuple-element.122.owners, bf16[1024,2048]{1,0:T(8,128)(2,1)S(1)} %copy-done.2, bf16[512,2048]{1,0:T(8,128)(2,1)S(1)} %get-tuple-element.119.panel, ...), custom_call_target="tpu_custom_call", output_to_operand_aliasing={{0}: (7, {}), {1}: (8, {})} | custom-call | tf_op jit(solution)/shard_map/gain/pallas_call | solution.py:254
  102.8 6.4 %collective-permute-done.30.refs_1_ = bf16[4,128,512]{2,1,0:T(8,128)(2,1)S(1)} collective-permute-done((bf16[4,128,512]{2,1,0:T(8,128)(2,1)S(1)}, bf16[4,128,512]{2,1,0:T(8,128)(2,1)S(1)}, u32[]{:S(2)}, u32[]{:S(2)}) %collective-permute-start.30) | collective-permute-done | bytes 524320 | tf_op jit(solution)/shard_map/ppermute | solution.py:57
  112.7 4.4 %gain.13 = (f32[4,1024,512]{2,1,0:T(8,128)S(1)}, f32[4,512,512]{2,1,0:T(8,128)S(1)}) custom-call(s32[16]{0:T(128)S(1)} %get-tuple-element.118.owners, bf16[1024,2048]{1,0:T(8,128)(2,1)S(1)} %copy-done.2, bf16[512,2048]{1,0:T(8,128)(2,1)S(1)} %get-tuple-element.119.panel, bf16[4,128,512]{2,1,0:T(8,128)(2,1)S(1)} %get-tuple-element.144.refs_0_, ...), custom_call_target="tpu_custom_call" | custom-call | tf_op jit(solution)/shard_map/gain/pallas_call | solution.py:254
  117.2 5.3 %gain.12 = (f32[4,1024,512]{2,1,0:T(8,128)S(1)}, f32[4,512,512]{2,1,0:T(8,128)S(1)}) custom-call(s32[16]{0:T(128)S(1)} %get-tuple-element.122.owners, bf16[1024,2048]{1,0:T(8,128)(2,1)S(1)} %copy-done.2, bf16[512,2048]{1,0:T(8,128)(2,1)S(1)} %get-tuple-element.119.panel, ...), custom_call_target="tpu_custom_call", output_to_operand_aliasing={{0}: (6, {}), {1}: (7, {})} | custom-call | tf_op jit(solution)/shard_map/gain/pallas_call | solution.py:254
  123.7 2.4 %collective-permute-done.36.refs_1_ = bf16[4,128,512]{2,1,0:T(8,128)(2,1)S(1)} collective-permute-done((bf16[4,128,512]{2,1,0:T(8,128)(2,1)S(1)}, bf16[4,128,512]{2,1,0:T(8,128)(2,1)S(1)}, u32[]{:S(2)}, u32[]{:S(2)}) %collective-permute-start.36) | collective-permute-done | bytes 524320 | tf_op jit(solution)/shard_map/ppermute | solution.py:57
  128.4 3.6 %gain.14 = (f32[4,1024,512]{2,1,0:T(8,128)S(1)}, f32[4,512,512]{2,1,0:T(8,128)S(1)}) custom-call(s32[16]{0:T(128)S(1)} %get-tuple-element.122.owners, bf16[1024,2048]{1,0:T(8,128)(2,1)S(1)} %copy-done.2, bf16[512,2048]{1,0:T(8,128)(2,1)S(1)} %get-tuple-element.119.panel, ...), custom_call_target="tpu_custom_call", output_to_operand_aliasing={{0}: (4, {}), {1}: (5, {})} | custom-call | tf_op jit(solution)/shard_map/gain/pallas_call | solution.py:254
  132.0 7.4 %close.2 = (f32[8,1024,512]{2,1,0:T(8,128)}, f32[8,128]{1,0:T(8,128)S(1)}) custom-call(f32[512,1]{1,0:T(8,128)S(1)} %get-tuple-element.117.column, f32[4,1024,512]{2,1,0:T(8,128)S(1)} %get-tuple-element.163.chi, f32[4,512,512]{2,1,0:T(8,128)S(1)} %get-tuple-element.164.step), custom_call_target="tpu_custom_call" | custom-call | tf_op jit(solution)/shard_map/close/pallas_call | solution.py:303
  144.2 8.5 %gain.15 = (f32[4,1024,512]{2,1,0:T(8,128)S(1)}, f32[4,512,512]{2,1,0:T(8,128)S(1)}) custom-call(s32[16]{0:T(128)S(1)} %get-tuple-element.118.owners, bf16[1024,2048]{1,0:T(8,128)(2,1)S(1)} %copy-done.2, bf16[512,2048]{1,0:T(8,128)(2,1)S(1)} %get-tuple-element.119.panel, ...), custom_call_target="tpu_custom_call", output_to_operand_aliasing={{0}: (10, {}), {1}: (11, {})} | custom-call | tf_op jit(solution)/shard_map/gain/pallas_call | solution.py:254
  152.7 3.6 %collective-permute-done.43.refs_0_ = bf16[4,128,512]{2,1,0:T(8,128)(2,1)S(1)} collective-permute-done((bf16[4,128,512]{2,1,0:T(8,128)(2,1)S(1)}, bf16[4,128,512]{2,1,0:T(8,128)(2,1)S(1)}, u32[]{:S(2)}, u32[]{:S(2)}) %collective-permute-start.43) | collective-permute-done | bytes 524320 | tf_op jit(solution)/shard_map/ppermute | solution.py:57
  158.1 5.4 %gain.16 = (f32[4,1024,512]{2,1,0:T(8,128)S(1)}, f32[4,512,512]{2,1,0:T(8,128)S(1)}) custom-call(s32[16]{0:T(128)S(1)} %get-tuple-element.118.owners, bf16[1024,2048]{1,0:T(8,128)(2,1)S(1)} %copy-done.2, bf16[512,2048]{1,0:T(8,128)(2,1)S(1)} %get-tuple-element.119.panel, ...), custom_call_target="tpu_custom_call", output_to_operand_aliasing={{0}: (7, {}), {1}: (8, {})} | custom-call | tf_op jit(solution)/shard_map/gain/pallas_call | solution.py:254
  163.5 3.7 %gain.17 = (f32[4,1024,512]{2,1,0:T(8,128)S(1)}, f32[4,512,512]{2,1,0:T(8,128)S(1)}) custom-call(s32[16]{0:T(128)S(1)} %get-tuple-element.118.owners, bf16[1024,2048]{1,0:T(8,128)(2,1)S(1)} %copy-done.2, bf16[512,2048]{1,0:T(8,128)(2,1)S(1)} %get-tuple-element.119.panel, ...), custom_call_target="tpu_custom_call", output_to_operand_aliasing={{0}: (5, {}), {1}: (6, {})} | custom-call | tf_op jit(solution)/shard_map/gain/pallas_call | solution.py:254
  167.3 8.0 %close.3 = (f32[8,1024,512]{2,1,0:T(8,128)}, f32[8,128]{1,0:T(8,128)}) custom-call(f32[512,1]{1,0:T(8,128)S(1)} %get-tuple-element.117.column, f32[4,1024,512]{2,1,0:T(8,128)S(1)} %get-tuple-element.184.chi, f32[4,512,512]{2,1,0:T(8,128)S(1)} %get-tuple-element.185.step, ...), custom_call_target="tpu_custom_call", output_to_operand_aliasing={{0}: (3, {})} | custom-call | tf_op jit(solution)/shard_map/close/pallas_call | solution.py:303
  (124 shorter events, 51.8 us)
Async XLA Ops:
  36.0 10.8 %collective-permute-start.18 = (bf16[8,128,128]{2,1,0:T(8,128)(2,1)S(1)}, bf16[8,128,128]{2,1,0:T(8,128)(2,1)S(1)}, u32[]{:S(2)}, u32[]{:S(2)}) collective-permute-start(bf16[8,128,128]{2,1,0:T(8,128)(2,1)S(1)} %fold.7.refs_3_), channel_id=1, source_target_pairs={{16,0},{0,16},{17,1},{1,17},{18,2},{2,18},{19,3},{3,19},{20,4},{4,... | collective-permute-start | bytes 786440 | tf_op jit(solution)/shard_map/ppermute | solution.py:359
  48.5 14.3 %collective-permute-start.20 = (bf16[4,128,512]{2,1,0:T(8,128)(2,1)S(1)}, bf16[4,128,512]{2,1,0:T(8,128)(2,1)S(1)}, u32[]{:S(2)}, u32[]{:S(2)}) collective-permute-start(bf16[4,128,512]{2,1,0:T(8,128)(2,1)S(1)} %get-tuple-element.113.refs_0_), channel_id=1, source_target_pairs={{4,0},{5,1},{8,4},{9,5},{12,8},{13,9},{14,12},{15,13},{10,14},{11,... | collective-permute-start | bytes 1572872 | tf_op jit(solution)/shard_map/ppermute | solution.py:57
  49.3 14.0 %collective-permute-start.19 = (bf16[4,128,512]{2,1,0:T(8,128)(2,1)S(1)}, bf16[4,128,512]{2,1,0:T(8,128)(2,1)S(1)}, u32[]{:S(2)}, u32[]{:S(2)}) collective-permute-start(bf16[4,128,512]{2,1,0:T(8,128)(2,1)S(1)} %get-tuple-element.113.refs_0_), channel_id=1, source_target_pairs={{0,4},{1,5},{4,8},{5,9},{8,12},{9,13},{12,14},{13,15},{14,10},{15,... | collective-permute-start | bytes 1572872 | tf_op jit(solution)/shard_map/ppermute | solution.py:57
  63.3 14.3 %collective-permute-start.22 = (bf16[4,128,512]{2,1,0:T(8,128)(2,1)S(1)}, bf16[4,128,512]{2,1,0:T(8,128)(2,1)S(1)}, u32[]{:S(2)}, u32[]{:S(2)}) collective-permute-start(bf16[4,128,512]{2,1,0:T(8,128)(2,1)S(1)} %collective-permute-done.19.refs_1_), channel_id=1, source_target_pairs={{0,4},{1,5},{4,8},{5,9},{8,12},{9,13},{12,14},{13,15},{14,10},{15,... | collective-permute-start | bytes 1572872 | tf_op jit(solution)/shard_map/ppermute | solution.py:57
  64.6 13.0 %collective-permute-start.25 = (bf16[4,128,512]{2,1,0:T(8,128)(2,1)S(1)}, bf16[4,128,512]{2,1,0:T(8,128)(2,1)S(1)}, u32[]{:S(2)}, u32[]{:S(2)}) collective-permute-start(bf16[4,128,512]{2,1,0:T(8,128)(2,1)S(1)} %collective-permute-done.20.refs_2_), channel_id=1, source_target_pairs={{0,1},{1,0},{2,3},{3,2},{4,5},{5,4},{6,7},{7,6},{8,9},{9,8},{10,11... | collective-permute-start | bytes 1572872 | tf_op jit(solution)/shard_map/ppermute | solution.py:52
  64.8 14.1 %collective-permute-start.23 = (bf16[4,128,512]{2,1,0:T(8,128)(2,1)S(1)}, bf16[4,128,512]{2,1,0:T(8,128)(2,1)S(1)}, u32[]{:S(2)}, u32[]{:S(2)}) collective-permute-start(bf16[4,128,512]{2,1,0:T(8,128)(2,1)S(1)} %collective-permute-done.20.refs_2_), channel_id=1, source_target_pairs={{4,0},{5,1},{8,4},{9,5},{12,8},{13,9},{14,12},{15,13},{10,14},{11,... | collective-permute-start | bytes 1572872 | tf_op jit(solution)/shard_map/ppermute | solution.py:57
  79.0 14.3 %collective-permute-start.26 = (bf16[4,128,512]{2,1,0:T(8,128)(2,1)S(1)}, bf16[4,128,512]{2,1,0:T(8,128)(2,1)S(1)}, u32[]{:S(2)}, u32[]{:S(2)}) collective-permute-start(bf16[4,128,512]{2,1,0:T(8,128)(2,1)S(1)} %collective-permute-done.22.refs_0_), channel_id=1, source_target_pairs={{0,4},{1,5},{4,8},{5,9},{8,12},{9,13},{12,14},{13,15},{14,10},{15,... | collective-permute-start | bytes 1572872 | tf_op jit(solution)/shard_map/ppermute | solution.py:57
  80.5 12.8 %collective-permute-start.29 = (bf16[4,128,512]{2,1,0:T(8,128)(2,1)S(1)}, bf16[4,128,512]{2,1,0:T(8,128)(2,1)S(1)}, u32[]{:S(2)}, u32[]{:S(2)}) collective-permute-start(bf16[4,128,512]{2,1,0:T(8,128)(2,1)S(1)} %collective-permute-done.23.refs_1_), channel_id=1, source_target_pairs={{0,1},{1,0},{2,3},{3,2},{4,5},{5,4},{6,7},{7,6},{8,9},{9,8},{10,11... | collective-permute-start | bytes 1572872 | tf_op jit(solution)/shard_map/ppermute | solution.py:52
  80.8 14.1 %collective-permute-start.27 = (bf16[4,128,512]{2,1,0:T(8,128)(2,1)S(1)}, bf16[4,128,512]{2,1,0:T(8,128)(2,1)S(1)}, u32[]{:S(2)}, u32[]{:S(2)}) collective-permute-start(bf16[4,128,512]{2,1,0:T(8,128)(2,1)S(1)} %collective-permute-done.23.refs_1_), channel_id=1, source_target_pairs={{4,0},{5,1},{8,4},{9,5},{12,8},{13,9},{14,12},{15,13},{10,14},{11,... | collective-permute-start | bytes 1572872 | tf_op jit(solution)/shard_map/ppermute | solution.py:57
  95.4 13.8 %collective-permute-start.30 = (bf16[4,128,512]{2,1,0:T(8,128)(2,1)S(1)}, bf16[4,128,512]{2,1,0:T(8,128)(2,1)S(1)}, u32[]{:S(2)}, u32[]{:S(2)}) collective-permute-start(bf16[4,128,512]{2,1,0:T(8,128)(2,1)S(1)} %get-tuple-element.144.refs_0_), channel_id=1, source_target_pairs={{4,0},{5,1},{8,4},{9,5},{12,8},{13,9},{14,12},{15,13},{10,14},{11,... | collective-permute-start | bytes 1572872 | tf_op jit(solution)/shard_map/ppermute | solution.py:57
  95.8 13.4 %collective-permute-start.33 = (bf16[4,128,512]{2,1,0:T(8,128)(2,1)S(1)}, bf16[4,128,512]{2,1,0:T(8,128)(2,1)S(1)}, u32[]{:S(2)}, u32[]{:S(2)}) collective-permute-start(bf16[4,128,512]{2,1,0:T(8,128)(2,1)S(1)} %collective-permute-done.26.refs_0_), channel_id=1, source_target_pairs={{0,1},{1,0},{2,3},{3,2},{4,5},{5,4},{6,7},{7,6},{8,9},{9,8},{10,11... | collective-permute-start | bytes 1572872 | tf_op jit(solution)/shard_map/ppermute | solution.py:52
  95.8 14.3 %collective-permute-start.31 = (bf16[4,128,512]{2,1,0:T(8,128)(2,1)S(1)}, bf16[4,128,512]{2,1,0:T(8,128)(2,1)S(1)}, u32[]{:S(2)}, u32[]{:S(2)}) collective-permute-start(bf16[4,128,512]{2,1,0:T(8,128)(2,1)S(1)} %collective-permute-done.26.refs_0_), channel_id=1, source_target_pairs={{0,4},{1,5},{4,8},{5,9},{8,12},{9,13},{12,14},{13,15},{14,10},{15,... | collective-permute-start | bytes 1572872 | tf_op jit(solution)/shard_map/ppermute | solution.py:57
  110.2 13.5 %collective-permute-start.35 = (bf16[4,128,512]{2,1,0:T(8,128)(2,1)S(1)}, bf16[4,128,512]{2,1,0:T(8,128)(2,1)S(1)}, u32[]{:S(2)}, u32[]{:S(2)}) collective-permute-start(bf16[4,128,512]{2,1,0:T(8,128)(2,1)S(1)} %get-tuple-element.144.refs_0_), channel_id=1, source_target_pairs={{0,4},{1,5},{4,8},{5,9},{8,12},{9,13},{12,14},{13,15},{14,10},{15,... | collective-permute-start | bytes 1572872 | tf_op jit(solution)/shard_map/ppermute | solution.py:57
  111.8 11.9 %collective-permute-start.37 = (bf16[4,128,512]{2,1,0:T(8,128)(2,1)S(1)}, bf16[4,128,512]{2,1,0:T(8,128)(2,1)S(1)}, u32[]{:S(2)}, u32[]{:S(2)}) collective-permute-start(bf16[4,128,512]{2,1,0:T(8,128)(2,1)S(1)} %collective-permute-done.31.refs_0_), channel_id=1, source_target_pairs={{0,1},{1,0},{2,3},{3,2},{4,5},{5,4},{6,7},{7,6},{8,9},{9,8},{10,11... | collective-permute-start | bytes 1572872 | tf_op jit(solution)/shard_map/ppermute | solution.py:52
  111.8 11.9 %collective-permute-start.38 = (bf16[4,128,512]{2,1,0:T(8,128)(2,1)S(1)}, bf16[4,128,512]{2,1,0:T(8,128)(2,1)S(1)}, u32[]{:S(2)}, u32[]{:S(2)}) collective-permute-start(bf16[4,128,512]{2,1,0:T(8,128)(2,1)S(1)} %collective-permute-done.30.refs_1_), channel_id=1, source_target_pairs={{0,1},{1,0},{2,3},{3,2},{4,5},{5,4},{6,7},{7,6},{8,9},{9,8},{10,11... | collective-permute-start | bytes 1572872 | tf_op jit(solution)/shard_map/ppermute | solution.py:52
  112.3 13.8 %collective-permute-start.36 = (bf16[4,128,512]{2,1,0:T(8,128)(2,1)S(1)}, bf16[4,128,512]{2,1,0:T(8,128)(2,1)S(1)}, u32[]{:S(2)}, u32[]{:S(2)}) collective-permute-start(bf16[4,128,512]{2,1,0:T(8,128)(2,1)S(1)} %collective-permute-done.30.refs_1_), channel_id=1, source_target_pairs={{4,0},{5,1},{8,4},{9,5},{12,8},{13,9},{14,12},{15,13},{10,14},{11,... | collective-permute-start | bytes 1572872 | tf_op jit(solution)/shard_map/ppermute | solution.py:57
  126.1 13.2 %collective-permute-start.41 = (bf16[4,128,512]{2,1,0:T(8,128)(2,1)S(1)}, bf16[4,128,512]{2,1,0:T(8,128)(2,1)S(1)}, u32[]{:S(2)}, u32[]{:S(2)}) collective-permute-start(bf16[4,128,512]{2,1,0:T(8,128)(2,1)S(1)} %collective-permute-done.35.refs_0_), channel_id=1, source_target_pairs={{0,1},{1,0},{2,3},{3,2},{4,5},{5,4},{6,7},{7,6},{8,9},{9,8},{10,11... | collective-permute-start | bytes 1572872 | tf_op jit(solution)/shard_map/ppermute | solution.py:52
  126.1 14.3 %collective-permute-start.39 = (bf16[4,128,512]{2,1,0:T(8,128)(2,1)S(1)}, bf16[4,128,512]{2,1,0:T(8,128)(2,1)S(1)}, u32[]{:S(2)}, u32[]{:S(2)}) collective-permute-start(bf16[4,128,512]{2,1,0:T(8,128)(2,1)S(1)} %collective-permute-done.35.refs_0_), channel_id=1, source_target_pairs={{0,4},{1,5},{4,8},{5,9},{8,12},{9,13},{12,14},{13,15},{14,10},{15,... | collective-permute-start | bytes 1572872 | tf_op jit(solution)/shard_map/ppermute | solution.py:57
  127.6 12.8 %collective-permute-start.42 = (bf16[4,128,512]{2,1,0:T(8,128)(2,1)S(1)}, bf16[4,128,512]{2,1,0:T(8,128)(2,1)S(1)}, u32[]{:S(2)}, u32[]{:S(2)}) collective-permute-start(bf16[4,128,512]{2,1,0:T(8,128)(2,1)S(1)} %collective-permute-done.36.refs_1_), channel_id=1, source_target_pairs={{0,1},{1,0},{2,3},{3,2},{4,5},{5,4},{6,7},{7,6},{8,9},{9,8},{10,11... | collective-permute-start | bytes 1572872 | tf_op jit(solution)/shard_map/ppermute | solution.py:52
  127.8 14.1 %collective-permute-start.40 = (bf16[4,128,512]{2,1,0:T(8,128)(2,1)S(1)}, bf16[4,128,512]{2,1,0:T(8,128)(2,1)S(1)}, u32[]{:S(2)}, u32[]{:S(2)}) collective-permute-start(bf16[4,128,512]{2,1,0:T(8,128)(2,1)S(1)} %collective-permute-done.36.refs_1_), channel_id=1, source_target_pairs={{4,0},{5,1},{8,4},{9,5},{12,8},{13,9},{14,12},{15,13},{10,14},{11,... | collective-permute-start | bytes 1572872 | tf_op jit(solution)/shard_map/ppermute | solution.py:57
  141.9 10.8 %collective-permute-start.45 = (bf16[4,128,512]{2,1,0:T(8,128)(2,1)S(1)}, bf16[4,128,512]{2,1,0:T(8,128)(2,1)S(1)}, u32[]{:S(2)}, u32[]{:S(2)}) collective-permute-start(bf16[4,128,512]{2,1,0:T(8,128)(2,1)S(1)} %collective-permute-done.39.refs_3_), channel_id=1, source_target_pairs={{0,1},{1,0},{2,3},{3,2},{4,5},{5,4},{6,7},{7,6},{8,9},{9,8},{10,11... | collective-permute-start | bytes 1572872 | tf_op jit(solution)/shard_map/ppermute | solution.py:52
  141.9 14.3 %collective-permute-start.43 = (bf16[4,128,512]{2,1,0:T(8,128)(2,1)S(1)}, bf16[4,128,512]{2,1,0:T(8,128)(2,1)S(1)}, u32[]{:S(2)}, u32[]{:S(2)}) collective-permute-start(bf16[4,128,512]{2,1,0:T(8,128)(2,1)S(1)} %collective-permute-done.39.refs_3_), channel_id=1, source_target_pairs={{0,4},{1,5},{4,8},{5,9},{8,12},{9,13},{12,14},{13,15},{14,10},{15,... | collective-permute-start | bytes 1572872 | tf_op jit(solution)/shard_map/ppermute | solution.py:57
  143.3 13.0 %collective-permute-start.46 = (bf16[4,128,512]{2,1,0:T(8,128)(2,1)S(1)}, bf16[4,128,512]{2,1,0:T(8,128)(2,1)S(1)}, u32[]{:S(2)}, u32[]{:S(2)}) collective-permute-start(bf16[4,128,512]{2,1,0:T(8,128)(2,1)S(1)} %collective-permute-done.40.refs_4_), channel_id=1, source_target_pairs={{0,1},{1,0},{2,3},{3,2},{4,5},{5,4},{6,7},{7,6},{8,9},{9,8},{10,11... | collective-permute-start | bytes 1572872 | tf_op jit(solution)/shard_map/ppermute | solution.py:52
  143.5 14.1 %collective-permute-start.44 = (bf16[4,128,512]{2,1,0:T(8,128)(2,1)S(1)}, bf16[4,128,512]{2,1,0:T(8,128)(2,1)S(1)}, u32[]{:S(2)}, u32[]{:S(2)}) collective-permute-start(bf16[4,128,512]{2,1,0:T(8,128)(2,1)S(1)} %collective-permute-done.40.refs_4_), channel_id=1, source_target_pairs={{4,0},{5,1},{8,4},{9,5},{12,8},{13,9},{14,12},{15,13},{10,14},{11,... | collective-permute-start | bytes 1572872 | tf_op jit(solution)/shard_map/ppermute | solution.py:57
  (29 other events, 218.3 us)
